TPU v7x, 512 devices: a whole 4x4x16 slice. The times are simulated.
512 devices in a mesh: ctx: 64 (over x, z), head: 8 (over y, core).
Axes of the slice: x: 4, y: 4, z: 16, core: 2. Of those that a mesh axis runs over, the one named last changes fastest.
Arguments:
- inputs: bfloat16 [16384, 4096], P(('ctx', 'head')), may hold values from -0.3125 to 0.3125
- step_sizes: bfloat16 [16384, 64], P(('ctx', 'head')), may hold values from 0 to 16384, as said below
- decay_rates: float32 [64], P('head'), may hold values from 0 to 1, as said below
- state_write: bfloat16 [16384, 512], P(('ctx', 'head')), may hold values from -6 to 6
- state_read: bfloat16 [16384, 512], P(('ctx', 'head')), may hold values from -0.75 to 0.75
- doc_lengths: int32 [16], replicated, may hold values from 1 to 8192, 16384 in all
- out_grad: bfloat16 [16384, 4096], P(('ctx', 'head')), may hold values from -0.3125 to 0.3125
Outputs:
- outputs: bfloat16 [16384, 4096], P(('ctx', 'head'))
- input_grad: bfloat16 [16384, 4096], P(('ctx', 'head'))
- write_grad: bfloat16 [16384, 512], P(('ctx', 'head'))
- read_grad: bfloat16 [16384, 512], P(('ctx', 'head'))
Inputs may be any that keep to these rules, and one draw needn't show every extreme that they name: `step_sizes`: positive steps; a few positions of the slab carry far larger steps than the others. `decay_rates`: positive rates. `doc_lengths`: the 16 lengths sum to 16384; the longest is exactly 8192.
All inputs are finite; a program needn't handle non-finite values.
Results may differ from a plain program's by a relative error of at most 0.012.
Values may be sent and summed in bfloat16 or wider, within the bound.
A program may use at most 128 MiB of HBM per device.

v0:
```python
import jax
import jax.numpy as jnp
from jax import lax
from jax.sharding import PartitionSpec as P

HEAD_DIM = 64
STATE = 64
BLOCK = 256


def carried_in(value, axis, join, neutral, backward):
    count, mine = (lax.axis_size(axis), lax.axis_index(axis))
    pieces = jax.tree.map(lambda part: lax.all_gather(part, axis), value)
    if backward:
        pieces = jax.tree.map(lambda part: part[::-1], pieces)
        mine = count - 1 - mine
    total = jax.tree.map(
        lambda part, zero: jnp.full_like(part, 0) + jnp.asarray(zero, part.dtype), value, neutral
    )

    def turn(position, total):
        longer = join(total, jax.tree.map(lambda part: part[position], pieces))
        return jax.tree.map(lambda new, old: jnp.where(position < mine, new, old), longer, total)

    return lax.fori_loop(0, count - 1, turn, total)


def segment_ids(doc_lengths, positions):
    ends = jnp.cumsum(doc_lengths)
    starts = ends - doc_lengths
    hits = (starts[None, :] <= positions[:, None]).astype(jnp.int32)
    return jnp.sum(hits, axis=1) - 1


def block_outputs(values, writers, readers, running, segment):
    scores = jnp.einsum("ign,jgn->gij", readers, writers, preferred_element_type=jnp.float32)
    levels = jnp.transpose(running, (1, 2, 0))
    spread = levels[:, :, :, None] - levels[:, :, None, :]
    length = segment.shape[0]
    row_index = lax.broadcasted_iota(jnp.int32, (length, length), 0)
    col_index = lax.broadcasted_iota(jnp.int32, (length, length), 1)
    allowed = (row_index >= col_index) & (segment[:, None] == segment[None, :])
    factor = jnp.where(allowed, jnp.exp(jnp.where(allowed, spread, 0.0)), 0.0)
    weights = (scores[:, None] * factor).astype(jnp.bfloat16)
    return jnp.einsum("ghij,jghp->ighp", weights, values, preferred_element_type=jnp.float32)


def carry_factor(running, segment, previous):
    return jnp.where((segment == previous)[:, None, None], jnp.exp(running), 0.0)


def carried_outputs(readers, running, segment, previous, carried):
    factor = carry_factor(running, segment, previous)
    product = jnp.einsum(
        "ign,ghnp->ighp", readers.astype(jnp.float32), carried, precision=lax.Precision.HIGHEST
    )
    return product * factor[..., None]


def block_state(values, writers, running, segment):
    final_sum = running[-1]
    allowed = segment == segment[-1]
    factor = jnp.where(allowed[:, None, None], jnp.exp(final_sum[None] - running), 0.0)
    weighted = (writers[:, :, None, :] * factor[..., None]).astype(jnp.bfloat16)
    return jnp.einsum("jghn,jghp->ghnp", weighted, values, preferred_element_type=jnp.float32)


def block_decay(running, segment, previous):
    return jnp.where(segment[-1] == previous, jnp.exp(running[-1]), 0.0)


def link_states(earlier, later):
    return (earlier[0] * later[0], later[0][..., None, None] * earlier[1] + later[1])


def fold_step(total, pieces):
    return (link_states(total, pieces), None)


def pass_step(carried, pieces):
    moved = link_states((jnp.ones_like(pieces[0]), carried), pieces)
    return (moved[1], carried)


def forward_chain(decays, states):
    identity = (jnp.ones_like(decays[0]), jnp.zeros_like(states[0]))
    device_pair, _ = lax.scan(fold_step, identity, (decays, states))
    entering = carried_in(device_pair, "ctx", link_states, identity, False)[1]
    _, entering_blocks = lax.scan(pass_step, entering, (decays, states))
    return entering_blocks


def backward_chain(decays, adjoint_blocks):
    identity = (jnp.ones_like(decays[0]), jnp.zeros_like(adjoint_blocks[0]))
    device_pair, _ = lax.scan(fold_step, identity, (decays, adjoint_blocks), reverse=True)
    leaving = carried_in(device_pair, "ctx", link_states, identity, True)[1]
    _, leaving_blocks = lax.scan(pass_step, leaving, (decays, adjoint_blocks), reverse=True)
    return leaving_blocks


def on_device(inputs, step_sizes, decay_rates, state_write, state_read, doc_lengths, out_grad):
    values, steps_local, writers, readers, cotangent = (
        lax.all_to_all(inputs, "head", split_axis=1, concat_axis=0, tiled=True),
        lax.all_to_all(step_sizes, "head", split_axis=1, concat_axis=0, tiled=True),
        lax.all_to_all(state_write, "head", split_axis=1, concat_axis=0, tiled=True),
        lax.all_to_all(state_read, "head", split_axis=1, concat_axis=0, tiled=True),
        lax.all_to_all(out_grad, "head", split_axis=1, concat_axis=0, tiled=True),
    )
    tokens_here = values.shape[0]
    heads_here = decay_rates.shape[0]
    groups_here = writers.shape[1] // STATE
    per_group = heads_here // groups_here
    blocks = tokens_here // BLOCK
    first_pos = lax.axis_index("ctx") * tokens_here
    positions = first_pos + jnp.arange(tokens_here, dtype=jnp.int32)
    segment = segment_ids(doc_lengths, positions).reshape(blocks, BLOCK)
    previous = segment_ids(doc_lengths, positions - 1).reshape(blocks, BLOCK)[:, 0]
    log_decay = -steps_local.astype(jnp.float32) * decay_rates[None, :]
    running = jnp.cumsum(log_decay.reshape(blocks, BLOCK, groups_here, per_group), axis=1)
    values = values.reshape(blocks, BLOCK, groups_here, per_group, HEAD_DIM)
    writers = writers.reshape(blocks, BLOCK, groups_here, STATE)
    readers = readers.reshape(blocks, BLOCK, groups_here, STATE)
    cotangent = cotangent.astype(jnp.float32).reshape(
        blocks, BLOCK, groups_here, per_group, HEAD_DIM
    )

    def local_part(some_values, some_writers, some_readers):

        def one_block(pieces):
            return block_outputs(pieces[0], pieces[1], pieces[2], pieces[3], pieces[4])

        return lax.map(one_block, (some_values, some_writers, some_readers, running, segment))

    def state_part(some_values, some_writers):
        return jax.vmap(block_state)(some_values, some_writers, running, segment)

    local_out, pull_local = jax.vjp(local_part, values, writers, readers)
    states, pull_states = jax.vjp(state_part, values, writers)
    decays = jax.vmap(block_decay)(running, segment, previous)
    entering_blocks = forward_chain(decays, states)

    def carry_part(some_readers, some_states):
        return jax.vmap(carried_outputs)(some_readers, running, segment, previous, some_states)

    carry_out, pull_carry = jax.vjp(carry_part, readers, entering_blocks)
    read_extra, adjoint_blocks = pull_carry(cotangent)
    leaving_blocks = backward_chain(decays, adjoint_blocks)
    result = (
        (local_out + carry_out).astype(jnp.bfloat16).reshape(tokens_here, heads_here * HEAD_DIM)
    )
    outputs = lax.all_to_all(result, "head", split_axis=0, concat_axis=1, tiled=True)
    values_local, writers_local, readers_local = pull_local(cotangent)
    values_state, writers_state = pull_states(leaving_blocks)
    input_grad = (values_local + values_state).reshape(tokens_here, heads_here * HEAD_DIM)
    write_grad = (writers_local + writers_state).reshape(tokens_here, groups_here * STATE)
    read_grad = (readers_local + read_extra).reshape(tokens_here, groups_here * STATE)
    input_grad, write_grad, read_grad = (
        lax.all_to_all(input_grad, "head", split_axis=0, concat_axis=1, tiled=True),
        lax.all_to_all(write_grad, "head", split_axis=0, concat_axis=1, tiled=True),
        lax.all_to_all(read_grad, "head", split_axis=0, concat_axis=1, tiled=True),
    )
    return (outputs, input_grad, write_grad, read_grad)


def solution(mesh):
    return jax.shard_map(
        on_device,
        mesh=mesh,
        in_specs=(
            P(("ctx", "head"), None),
            P(("ctx", "head"), None),
            P("head"),
            P(("ctx", "head"), None),
            P(("ctx", "head"), None),
            P(),
            P(("ctx", "head"), None),
        ),
        out_specs=(
            P(("ctx", "head"), None),
            P(("ctx", "head"), None),
            P(("ctx", "head"), None),
            P(("ctx", "head"), None),
        ),
        check_vma=False,
    )
```

profile of v0, /device:TPU:1, one launch (start us, length us, event | category | flops | bytes accessed | tf_op | source)
XLA Modules:
  0.0 545.3 jit_solution(12446991779789385122)
XLA Ops:
  8.6 10.1 %all-to-all-start.2 = ((bf16[8,2,128]{2,1,0:T(2,128)(2,1)}), bf16[8,2,128]{2,1,0:T(2,128)(2,1)S(1)}, u32[]{:S(2)}, u32[]{:S(2)}) async-start(bf16[8,2,128]{2,1,0:T(2,128)(2,1)} %reshape.502), calls=%async_computation.2 | async-start | bytes 8192 | tf_op jit(solution)/shard_map/all_to_all | solution.py:104
  21.5 1.3 broadcast_compare_fusion.1
  24.1 1.7 copy.167
  27.4 4.8 all-to-all-start
  34.0 3.0 all-to-all-done
  36.9 4.0 all-to-all-start.5
  41.3 6.2 %all-to-all-done.5 = bf16[32,8,512]{2,0,1:T(8,128)(2,1)S(1)} async-done(((bf16[32,8,512]{2,0,1:T(8,128)(2,1)}), bf16[32,8,512]{2,0,1:T(8,128)(2,1)S(1)}, u32[]{:S(2)}, u32[]{:S(2)}) %all-to-all-start.5) | async-done | bytes 262176 | tf_op jit(solution)/shard_map/all_to_all | solution.py:107
  50.3 4.3 all-to-all-start.1
  55.6 67.2 %all-gather = f32[64,1,1,8]{3,2,1,0:T(1,128)S(1)} all-gather(f32[1,1,1,8]{3,2,1,0:T(1,128)S(1)} %copy.128), channel_id=2, replica_groups=mesh['ctx'=64,'head'=8] {'ctx'}, dimensions={0}, use_global_device_ids=true | all-gather | bytes 2080 | tf_op jit(solution)/shard_map/all_gather | solution.py:13
  123.1 13.4 %all-to-all-start.3 = ((bf16[32,8,512]{2,0,1:T(8,128)(2,1)}), bf16[32,8,512]{2,0,1:T(8,128)(2,1)S(1)}, u32[]{:S(2)}, u32[]{:S(2)}) async-start(bf16[32,8,512]{2,0,1:T(8,128)(2,1)} %bitcast.228), calls=%async_computation.3 | async-start | bytes 524288 | tf_op jit(solution)/shard_map/all_to_all | solution.py:103
  137.0 6.1 %all-to-all-done.3 = bf16[32,8,512]{2,0,1:T(8,128)(2,1)S(1)} async-done(((bf16[32,8,512]{2,0,1:T(8,128)(2,1)}), bf16[32,8,512]{2,0,1:T(8,128)(2,1)S(1)}, u32[]{:S(2)}, u32[]{:S(2)}) %all-to-all-start.3) | async-done | bytes 262176 | tf_op jit(solution)/shard_map/all_to_all | solution.py:103
  146.1 95.4 %all-gather.5.cloned.1.call-done = f32[64,1,8,64,64]{4,3,2,1,0:T(8,128)} async-done(((f32[1,1,8,64,64]{4,3,2,1,0:T(8,128)}), f32[64,1,8,64,64]{4,3,2,1,0:T(8,128)}) %all-gather.5.cloned.1.call-update) | async-done | bytes 8388624 | tf_op jit(solution)/shard_map/all_gather | solution.py:13
  241.5 11.8 %rev.7 = f32[64,1,8,64,64]{4,3,2,1,0:T(8,128)} reverse(f32[64,1,8,64,64]{4,3,2,1,0:T(8,128)} %all-gather.5.cloned.1.call-done), dimensions={0} | reverse | bytes 16777216 | tf_op jit(solution)/shard_map/rev | solution.py:15
  253.2 68.8 %while.21 = (s32[]{:T(128)}, f32[1,8,64,64]{3,2,1,0:T(8,128)S(1)}, s32[]{:T(128)}, f32[64,1,8]{2,1,0:T(1,128)S(1)}, f32[64,1,8,64,64]{4,3,2,1,0:T(8,128)}, /*index=5*/s32[]{:T(128)}, s32[]{:T(128)}) while((s32[]{:T(128)}, f32[1,8,64,64]{3,2,1,0:T(8,128)S(1)}, s32[]{:T(128)}, f32[64,1,8]{2,1,0:T(1,128)S(1)}, ...), condition=%wide.region_8.9_spmd.clone, body=%wide.region_7.8_spmd.clone.sunk | while | flops 131076 | bytes 393417 | solution.py:25
  264.1 1.1 fusion.67
  323.3 5.4 all-to-all-start.7
  329.0 106.2 %all-gather.7.cloned.1.call-done = f32[512,64,64]{2,1,0:T(8,128)} async-done(((f32[8,64,64]{2,1,0:T(8,128)}), f32[512,64,64]{2,1,0:T(8,128)}) %all-gather.7.cloned.1.call-update) | async-done | bytes 8388624 | tf_op jit(solution)/shard_map/all_gather | solution.py:13
  435.2 68.7 %while.20 = (s32[]{:T(128)}, f32[1,8,64,64]{3,2,1,0:T(8,128)S(1)}, s32[]{:T(128)}, f32[64,1,8]{2,1,0:T(1,128)S(1)}, f32[64,1,8,64,64]{4,3,2,1,0:T(8,128)}, /*index=5*/s32[]{:T(128)}, s32[]{:T(128)}) while((s32[]{:T(128)}, f32[1,8,64,64]{3,2,1,0:T(8,128)S(1)}, s32[]{:T(128)}, f32[64,1,8]{2,1,0:T(1,128)S(1)}, ...), condition=%wide.region_6.7_spmd.clone, body=%wide.region_5.6_spmd.clone.sunk | while | flops 131076 | bytes 393417 | solution.py:25
  506.2 5.4 all-to-all-start.8
  513.3 2.9 all-to-all-done.8
  516.3 4.0 all-to-all-start.6
  522.5 4.4 all-to-all-done.6
  526.9 4.4 all-to-all-start.4
  533.7 4.0 all-to-all-done.4
  (344 shorter events, 158.6 us)
Async XLA Ops:
  8.6 18.7 %all-to-all-start.2 = ((bf16[8,2,128]{2,1,0:T(2,128)(2,1)}), bf16[8,2,128]{2,1,0:T(2,128)(2,1)S(1)}, u32[]{:S(2)}, u32[]{:S(2)}) async-start(bf16[8,2,128]{2,1,0:T(2,128)(2,1)} %reshape.502), calls=%async_computation.2 | async-start | bytes 8192 | tf_op jit(solution)/shard_map/all_to_all | solution.py:104
  27.4 9.5 %all-to-all-start = ((bf16[8,2,1024]{2,1,0:T(2,128)(2,1)}), bf16[8,2,1024]{2,1,0:T(2,128)(2,1)S(1)}, u32[]{:S(2)}, u32[]{:S(2)}) async-start(bf16[8,2,1024]{2,1,0:T(2,128)(2,1)} %reshape.500), calls=%async_computation | async-start | bytes 65536 | tf_op jit(solution)/shard_map/all_to_all | solution.py:106
  36.9 10.6 %all-to-all-start.5 = ((bf16[32,8,512]{2,0,1:T(8,128)(2,1)}), bf16[32,8,512]{2,0,1:T(8,128)(2,1)S(1)}, u32[]{:S(2)}, u32[]{:S(2)}) async-start(bf16[32,8,512]{2,0,1:T(8,128)(2,1)} %bitcast.227), calls=%async_computation.5 | async-start | bytes 524288 | tf_op jit(solution)/shard_map/all_to_all | solution.py:107
  41.0 200.5 %all-gather.5.cloned.1.call-start = ((), (), s32[]{:S(2)}) async-start(), calls=%async_computation.9 | async-start | bytes 17039360 | tf_op jit(solution)/shard_map/all_gather | solution.py:13
  47.6 1.9 copy-start.1
  47.8 6.8 %copy-start = (bf16[32,4096]{1,0:T(8,128)(2,1)S(1)}, bf16[32,4096]{1,0:T(8,128)(2,1)}, u32[]{:S(2)}) copy-start(bf16[32,4096]{1,0:T(8,128)(2,1)} %param.11) | copy-start | bytes 786436
  50.3 72.8 %all-to-all-start.1 = ((bf16[8,2,1024]{2,1,0:T(2,128)(2,1)}), bf16[8,2,1024]{2,1,0:T(2,128)(2,1)S(1)}, u32[]{:S(2)}, u32[]{:S(2)}) async-start(bf16[8,2,1024]{2,1,0:T(2,128)(2,1)} %reshape.504), calls=%async_computation.1 | async-start | bytes 65536 | tf_op jit(solution)/shard_map/all_to_all | solution.py:105
  123.1 20.0 %all-to-all-start.3 = ((bf16[32,8,512]{2,0,1:T(8,128)(2,1)}), bf16[32,8,512]{2,0,1:T(8,128)(2,1)S(1)}, u32[]{:S(2)}, u32[]{:S(2)}) async-start(bf16[32,8,512]{2,0,1:T(8,128)(2,1)} %bitcast.228), calls=%async_computation.3 | async-start | bytes 524288 | tf_op jit(solution)/shard_map/all_to_all | solution.py:103
  136.6 298.6 %all-gather.7.cloned.1.call-start = ((), (), s32[]{:S(2)}) async-start(), calls=%async_computation.10 | async-start | bytes 17039360 | tf_op jit(solution)/shard_map/all_gather | solution.py:13
  323.3 182.9 %all-to-all-start.7 = ((bf16[8,2,1024]{2,1,0:T(2,128)(2,1)}), bf16[8,2,1024]{2,1,0:T(2,128)(2,1)S(1)}, u32[]{:S(2)}, u32[]{:S(2)}) async-start(bf16[8,2,1024]{2,1,0:T(2,128)(2,1)} %reshape.506), calls=%async_computation.7 | async-start | bytes 65536 | tf_op jit(solution)/shard_map/all_to_all | solution.py:159
  506.2 10.1 %all-to-all-start.8 = ((bf16[8,2,1024]{2,1,0:T(2,128)(2,1)}), bf16[8,2,1024]{2,1,0:T(2,128)(2,1)S(1)}, u32[]{:S(2)}, u32[]{:S(2)}) async-start(bf16[8,2,1024]{2,1,0:T(2,128)(2,1)} %reshape.508), calls=%async_computation.8 | async-start | bytes 65536 | tf_op jit(solution)/shard_map/all_to_all | solution.py:160
  516.3 10.6 %all-to-all-start.6 = ((bf16[8,32,512]{2,1,0:T(8,128)(2,1)}), bf16[8,32,512]{2,1,0:T(8,128)(2,1)S(1)}, u32[]{:S(2)}, u32[]{:S(2)}) async-start(bf16[8,32,512]{2,1,0:T(8,128)(2,1)} %all_to_all.130), calls=%async_computation.6 | async-start | bytes 524288 | tf_op jit(solution)/shard_map/all_to_all | solution.py:158
  526.9 10.9 %all-to-all-start.4 = ((bf16[8,32,512]{2,1,0:T(8,128)(2,1)}), bf16[8,32,512]{2,1,0:T(8,128)(2,1)S(1)}, u32[]{:S(2)}, u32[]{:S(2)}) async-start(bf16[8,32,512]{2,1,0:T(8,128)(2,1)} %all_to_all.123), calls=%async_computation.4 | async-start | bytes 524288 | tf_op jit(solution)/shard_map/all_to_all | solution.py:151
Sparse Core Ops, SparseCore 0:
  49.5 191.8 all-gather.4
  245.0 190.1 all-gather.6
where the time goes:
time: 550 us; the launch traced here: 545 us
  waiting for transfers between devices  228 us (41%)
  other arithmetic  137 us (25%)
  blocking collectives  67.2 us (12%)
  starting transfers between devices  55.8 us (10%)
  local copies, waits for them, and re-layouts  32 us (6%)
  between operations  15.6 us (3%)
  matrix products  5.53 us (1%)
    all_gather x2, waiting for transfers between devices, carried_in(): pieces = jax.tree.map(lambda part: lax.all_gather(part, axis), value)  202 us
    select_n x126, other arithmetic, turn(): jnp.where(position < mine, new, old)  133 us
    all_gather x1, blocking collectives, carried_in(): pieces = jax.tree.map(lambda part: lax.all_gather(part, axis), value)  67.2 us
    all_to_all x1, starting transfers between devices, on_device(): lax.all_to_all(inputs, 'head', split_axis=1, concat_axis=0, tiled=True)  13.4 us
    rev x2, local copies, waits for them, and re-layouts, carried_in(): pieces = jax.tree.map(lambda part: part[::-1], pieces)  11.8 us
  transfers between devices with their start and end apart: 11, of which 8 were waited for; matrix products, arithmetic and copies ran while one was open for 30% of the time, Pallas kernels for 0%

commit v1 on v0

v1 whole, which is shorter than its diff:
```python
import functools

import jax
import jax.numpy as jnp
from jax import lax
from jax.experimental import pallas as pl
from jax.experimental.pallas import tpu as pltpu
from jax.sharding import PartitionSpec as P

HEAD_DIM = 64
STATE = 64
BLOCK = 256
DOCS = 16
HEADS_HERE = 8
WIDE = HEADS_HERE * HEAD_DIM
PAIRS = HEADS_HERE // 2
LANES = 128
NEG = -1e30
F32 = jnp.float32
BF16 = jnp.bfloat16


def dot_nn(a, b):
    return lax.dot_general(a, b, (((1,), (0,)), ((), ())), preferred_element_type=F32)


def dot_nt(a, b):
    return lax.dot_general(a, b, (((1,), (1,)), ((), ())), preferred_element_type=F32)


def dot_tn(a, b):
    return lax.dot_general(a, b, (((0,), (0,)), ((), ())), preferred_element_type=F32)


def kernel(
    nx, nz, ny,
    x_ref, step_ref, rate_ref, w_ref, r_ref, doc_ref, g_ref,
    out_ref, dx_ref, dw_ref, dr_ref,
    st_send, st_buf, wr_send, wr_buf, v_buf, g_buf,
    dec_send, dec_recv, f_send, f_recv, b_send, b_recv,
    xf_send, xf_recv, xb_send, xb_recv,
    rf_send, rf_recv, rb_send, rb_recv,
    out_send, dx_send, gw_send, gw_recv,
    run_col, run_row, bias_ref, score_ref, dscore_ref, ev_ref, cg_ref, loc_ref, dv_ref,
    y_ssem, y_rsem, z_ssem, z_rsem, x_ssem, x_rsem, own_sem,
):
    rows = BLOCK // ny
    blocks_of = nz // PAIRS
    piece = STATE // blocks_of
    ctx = lax.axis_index("ctx")
    me = lax.axis_index("head")
    zme = lax.rem(ctx, nz)
    xme = lax.div(ctx, nz)
    base = xme * nz

    def y_peer(k):
        return lax.rem(me + k, ny)

    def y_from(k):
        return lax.rem(me + ny - k, ny)

    def z_peer(k):
        return lax.rem(zme + k, nz)

    def z_from(k):
        return lax.rem(zme + nz - k, nz)

    def x_peer(k):
        return lax.rem(xme + k, nx)

    def x_from(k):
        return lax.rem(xme + nx - k, nx)

    def y_copy(cat, k, src, dst):
        return pltpu.make_async_remote_copy(
            src_ref=src, dst_ref=dst, send_sem=y_ssem.at[cat, k], recv_sem=y_rsem.at[cat, k],
            device_id={"ctx": ctx, "head": y_peer(k)}, device_id_type=pl.DeviceIdType.MESH)

    def z_copy(cat, k, src, dst):
        return pltpu.make_async_remote_copy(
            src_ref=src, dst_ref=dst, send_sem=z_ssem.at[cat, k], recv_sem=z_rsem.at[cat, k],
            device_id={"ctx": base + z_peer(k), "head": me}, device_id_type=pl.DeviceIdType.MESH)

    def x_copy(cat, k, src, dst):
        return pltpu.make_async_remote_copy(
            src_ref=src, dst_ref=dst, send_sem=x_ssem.at[cat, k], recv_sem=x_rsem.at[cat, k],
            device_id={"ctx": x_peer(k) * nz + zme, "head": me}, device_id_type=pl.DeviceIdType.MESH)

    def wide(at):
        return pl.ds(pl.multiple_of(at * WIDE, WIDE), WIDE)

    def z_offset(i):
        half = lax.div(i + 1, 2)
        return nz // 2 + half * (1 - 2 * lax.rem(i, 2))

    def each(count, body):
        def step(i, carry):
            body(i)
            return carry

        lax.fori_loop(0, count, step, 0)

    barrier = pltpu.get_barrier_semaphore()
    each(ny - 1, lambda i: pl.semaphore_signal(
        barrier, inc=1, device_id={"ctx": ctx, "head": y_peer(i + 1)}, device_id_type=pl.DeviceIdType.MESH))
    each(nx - 1, lambda i: pl.semaphore_signal(
        barrier, inc=1, device_id={"ctx": x_peer(i + 1) * nz + zme, "head": me}, device_id_type=pl.DeviceIdType.MESH))
    each(nz - 1, lambda i: pl.semaphore_signal(
        barrier, inc=1, device_id={"ctx": base + z_peer(i + 1), "head": me}, device_id_type=pl.DeviceIdType.MESH))

    own_v = pltpu.make_async_copy(x_ref.at[:, wide(me)], v_buf.at[me], own_sem.at[0])
    own_g = pltpu.make_async_copy(g_ref.at[:, wide(me)], g_buf.at[me], own_sem.at[1])
    own_v.start()
    own_g.start()
    low = lax.broadcasted_iota(jnp.int32, (rows, LANES), 1) < 64
    st_send[...] = jnp.zeros((rows, LANES), BF16)
    st_send[:, 0:ny * HEADS_HERE] = step_ref[...]
    for pair in range(ny // 2):
        cols = slice(pair * LANES, (pair + 1) * LANES)
        w2 = w_ref[:, cols].astype(F32)
        r2 = r_ref[:, cols].astype(F32)
        wr_send[2 * pair] = jnp.where(low, w2, pltpu.roll(r2, 64, 1)).astype(BF16)
        wr_send[2 * pair + 1] = jnp.where(low, pltpu.roll(w2, 64, 1), r2).astype(BF16)
    st_buf[me] = st_send[...]
    wr_buf[me] = wr_send[me]

    first = ctx * BLOCK
    starts, at = [], jnp.int32(0)
    for k in range(DOCS):
        starts.append(at)
        at = at + doc_ref[k]

    def segment(pos):
        seg = jnp.where(starts[0] <= pos, 1, 0)
        for k in range(1, DOCS):
            seg = seg + jnp.where(starts[k] <= pos, 1, 0)
        return seg

    seg_before = segment(first - 1)
    seg_last = segment(first + BLOCK - 1)
    seg_col = segment(first + lax.broadcasted_iota(jnp.int32, (BLOCK, LANES), 0))
    seg_row = segment(first + lax.broadcasted_iota(jnp.int32, (8, BLOCK), 1))[0:1]
    row_i = lax.broadcasted_iota(jnp.int32, (BLOCK, BLOCK), 0)
    col_i = lax.broadcasted_iota(jnp.int32, (BLOCK, BLOCK), 1)
    causal = row_i >= col_i
    seg_wide = jnp.concatenate([seg_col, seg_col], axis=1)
    bias_ref[...] = jnp.where(causal & (seg_wide == seg_row), 0.0, NEG)
    through = jnp.where(seg_last == seg_before, 1.0, 0.0)
    pl.semaphore_wait(barrier, ny - 1 + nz - 1 + nx - 1)

    def send_small(i):
        y_copy(0, i + 1, st_send, st_buf.at[me]).start()
        y_copy(1, i + 1, wr_send.at[y_peer(i + 1)], wr_buf.at[me]).start()

    each(ny - 1, send_small)
    each(ny - 1, lambda i: y_copy(2, i + 1, x_ref.at[:, wide(y_peer(i + 1))], v_buf.at[me]).start())
    each(ny - 1, lambda i: y_copy(3, i + 1, g_ref.at[:, wide(y_peer(i + 1))], g_buf.at[me]).start())

    each(ny - 1, lambda i: y_copy(0, i + 1, st_send, st_buf.at[y_from(i + 1)]).wait_recv())
    steps = st_buf[...].reshape(BLOCK, LANES)
    pick = (lax.broadcasted_iota(jnp.int32, (LANES, HEADS_HERE * LANES), 0) == me * HEADS_HERE
            + lax.broadcasted_iota(jnp.int32, (LANES, HEADS_HERE * LANES), 1) // LANES)
    spread_steps = dot_nn(steps, jnp.where(pick, 1.0, 0.0).astype(BF16)).astype(BF16)
    summed = dot_nn(jnp.where(causal, 1.0, 0.0).astype(BF16), spread_steps)
    pick_row = (lax.broadcasted_iota(jnp.int32, (16, LANES), 1) == me * HEADS_HERE
                + lax.broadcasted_iota(jnp.int32, (16, LANES), 0))
    steps_row = dot_nt(jnp.where(pick_row, 1.0, 0.0).astype(BF16), steps).astype(BF16)
    summed_row = dot_nn(steps_row, jnp.where(row_i <= col_i, 1.0, 0.0).astype(BF16))
    for h in range(HEADS_HERE):
        run_col[:, h * LANES:(h + 1) * LANES] = summed[:, h * LANES:(h + 1) * LANES] * (-rate_ref[h])
        run_row[h:h + 1, :] = summed_row[h:h + 1, :] * (-rate_ref[h])
    low = lax.broadcasted_iota(jnp.int32, (BLOCK, LANES), 1) < 64
    low_row = low[0:1]

    def pair_run(t):
        return jnp.where(low, run_col[:, 2 * t * LANES:(2 * t + 1) * LANES],
                         run_col[:, (2 * t + 1) * LANES:(2 * t + 2) * LANES])

    def pair_last(t):
        return jnp.where(low_row, run_col[BLOCK - 1:BLOCK, 2 * t * LANES:(2 * t + 1) * LANES],
                         run_col[BLOCK - 1:BLOCK, (2 * t + 1) * LANES:(2 * t + 2) * LANES])

    def factor_in(t):
        return jnp.where(seg_col == seg_before, jnp.exp(pair_run(t)), 0.0)

    def factor_out(t):
        return jnp.where(seg_col == seg_last, jnp.exp(pair_last(t) - pair_run(t)), 0.0)

    for t in range(PAIRS):
        dec_send[t] = jnp.exp(pair_last(t)) * through
    dec_recv[zme] = dec_send[zme // blocks_of]

    def send_decay(i):
        k = z_offset(i)
        z_copy(0, k, dec_send.at[lax.div(z_peer(k), blocks_of)], dec_recv.at[zme]).start()

    each(nz - 1, send_decay)

    each(ny - 1, lambda i: y_copy(1, i + 1, wr_send.at[y_peer(i + 1)], wr_buf.at[y_from(i + 1)]).wait_recv())
    wr = wr_buf[...].reshape(BLOCK, LANES)
    rw = pltpu.roll(wr.astype(F32), 64, 1)
    writers = wr[:, 0:64]
    readers = rw[:, 0:64].astype(BF16)
    read_low = jnp.where(low, rw, 0.0).astype(BF16)
    write_high = jnp.where(low, 0.0, rw).astype(BF16)
    score_ref[...] = dot_nt(readers, writers)

    own_v.wait()
    each(ny - 1, lambda i: y_copy(2, i + 1, x_ref.at[:, wide(y_peer(i + 1))], v_buf.at[y_from(i + 1)]).wait_recv())
    for t in range(PAIRS):
        cols = slice(t * LANES, (t + 1) * LANES)
        values = v_buf[:, :, cols].reshape(BLOCK, LANES)
        ev = (values.astype(F32) * factor_out(t)).astype(BF16)
        ev_ref[:, cols] = ev
        added = dot_tn(wr, ev)[0:STATE].astype(BF16)
        f_send[t * blocks_of:(t + 1) * blocks_of] = added.reshape(blocks_of, piece, LANES)

    def send_f(i):
        k = z_offset(i)
        z_copy(1, k, f_send.at[z_peer(k)], f_recv.at[zme]).start()

    each(nz - 1, send_f)
    f_recv[zme] = f_send[zme]

    own_g.wait()
    each(ny - 1, lambda i: y_copy(3, i + 1, g_ref.at[:, wide(y_peer(i + 1))], g_buf.at[y_from(i + 1)]).wait_recv())
    for t in range(PAIRS):
        cols = slice(t * LANES, (t + 1) * LANES)
        grads = g_buf[:, :, cols].reshape(BLOCK, LANES)
        cg = (grads.astype(F32) * factor_in(t)).astype(BF16)
        cg_ref[:, cols] = cg
        added = dot_tn(wr, cg)[STATE:2 * STATE].astype(BF16)
        b_send[t * blocks_of:(t + 1) * blocks_of] = added.reshape(blocks_of, piece, LANES)

    def send_b(i):
        k = z_offset(i)
        z_copy(2, k, b_send.at[z_peer(k)], b_recv.at[zme]).start()

    each(nz - 1, send_b)
    b_recv[zme] = b_send[zme]

    dscore_ref[...] = jnp.zeros((BLOCK, BLOCK), F32)
    low_one = jnp.where(low_row, 1.0, 0.0).astype(BF16)
    high_one = jnp.where(low_row, 0.0, 1.0).astype(BF16)

    def inside(t, carry):
        cols = pl.ds(pl.multiple_of(t * LANES, LANES), LANES)
        values = v_buf[:, :, cols].reshape(BLOCK, LANES)
        grads = g_buf[:, :, cols].reshape(BLOCK, LANES)
        local = jnp.zeros((BLOCK, LANES), F32)
        dvalue = jnp.zeros((BLOCK, LANES), F32)
        for half, ones in ((0, low_one), (1, high_one)):
            h = 2 * t + half
            column = run_col[:, pl.ds(pl.multiple_of(h * LANES, LANES), LANES)]
            row = run_row[pl.ds(h, 1), :]
            factor = jnp.exp(jnp.concatenate([column, column], axis=1) - row + bias_ref[...])
            weights = (score_ref[...] * factor).astype(BF16)
            half_grads = grads * ones
            local = local + dot_nn(weights, values * ones)
            dscore_ref[...] += dot_nt(half_grads, values) * factor
            dvalue = dvalue + dot_tn(weights, half_grads)
        loc_ref[:, cols] = local
        dv_ref[:, cols] = dvalue
        return carry

    lax.fori_loop(0, 2, inside, 0)

    each(nz - 1, lambda i: z_copy(0, i + 1, dec_send.at[0], dec_recv.at[z_from(i + 1)]).wait_recv())
    each(nz - 1, lambda i: z_copy(1, i + 1, f_send.at[0], f_recv.at[z_from(i + 1)]).wait_recv())
    total = jnp.zeros((piece, LANES), F32)
    product = jnp.ones((1, LANES), F32)
    for z in range(nz):
        total = dec_recv[z] * total + f_recv[z].astype(F32)
        product = dec_recv[z] * product
    xf_send[0:piece] = total
    xf_send[piece:piece + 8] = jnp.broadcast_to(product, (8, LANES))
    each(nx - 1, lambda i: x_copy(0, i + 1, xf_send, xf_recv.at[xme]).start())
    xf_recv[xme] = xf_send[...]
    each(nz - 1, lambda i: z_copy(2, i + 1, b_send.at[0], b_recv.at[z_from(i + 1)]).wait_recv())
    total = jnp.zeros((piece, LANES), F32)
    for z in reversed(range(nz)):
        total = dec_recv[z] * total + b_recv[z].astype(F32)
    xb_send[...] = total
    each(nx - 1, lambda i: x_copy(1, i + 1, xb_send, xb_recv.at[xme]).start())
    xb_recv[xme] = xb_send[...]

    lax.fori_loop(2, 3, inside, 0)

    each(nx - 1, lambda i: x_copy(0, i + 1, xf_send, xf_recv.at[x_from(i + 1)]).wait_recv())
    state = jnp.zeros((piece, LANES), F32)
    for x in range(nx):
        longer = xf_recv[x, piece:piece + 1] * state + xf_recv[x, 0:piece]
        state = jnp.where(x < xme, longer, state)
    for z in range(nz):
        rf_send[z] = state.astype(BF16)
        state = dec_recv[z] * state + f_recv[z].astype(F32)

    def return_f(i):
        k = z_offset(i)
        z_copy(3, k, rf_send.at[z_peer(k)], rf_recv.at[zme]).start()

    each(nz - 1, return_f)
    rf_recv[zme] = rf_send[zme]

    each(nx - 1, lambda i: x_copy(1, i + 1, xb_send, xb_recv.at[x_from(i + 1)]).wait_recv())
    state = jnp.zeros((piece, LANES), F32)
    for x in reversed(range(nx)):
        longer = xf_recv[x, piece:piece + 1] * state + xb_recv[x]
        state = jnp.where(x > xme, longer, state)
    for z in reversed(range(nz)):
        rb_send[z] = state.astype(BF16)
        state = dec_recv[z] * state + b_recv[z].astype(F32)

    def return_b(i):
        k = z_offset(i)
        z_copy(4, k, rb_send.at[z_peer(k)], rb_recv.at[zme]).start()

    each(nz - 1, return_b)
    rb_recv[zme] = rb_send[zme]

    lax.fori_loop(3, 4, inside, 0)
    dscore = dscore_ref[...].astype(BF16)
    gw = dot_nn(dscore, write_high) + dot_tn(dscore, read_low)
    nothing = jnp.zeros((STATE, LANES), BF16)

    each(nz - 1, lambda i: z_copy(3, i + 1, rf_send.at[0], rf_recv.at[z_from(i + 1)]).wait_recv())
    for t in range(PAIRS):
        cols = slice(t * LANES, (t + 1) * LANES)
        entering = rf_recv[t * blocks_of:(t + 1) * blocks_of].reshape(STATE, LANES)
        result = loc_ref[:, cols] + factor_in(t) * dot_nn(readers, entering)
        out_send[:, :, cols] = result.astype(BF16).reshape(ny, rows, LANES)
        gw = gw + dot_nt(cg_ref[:, cols], jnp.concatenate([nothing, entering], axis=0))
    each(ny - 1, lambda i: y_copy(4, i + 1, out_send.at[y_peer(i + 1)], out_ref.at[:, wide(me)]).start())
    own_out = pltpu.make_async_copy(out_send.at[me], out_ref.at[:, wide(me)], own_sem.at[2])
    own_out.start()

    each(nz - 1, lambda i: z_copy(4, i + 1, rb_send.at[0], rb_recv.at[z_from(i + 1)]).wait_recv())
    for t in range(PAIRS):
        cols = slice(t * LANES, (t + 1) * LANES)
        leaving = rb_recv[t * blocks_of:(t + 1) * blocks_of].reshape(STATE, LANES)
        result = dv_ref[:, cols] + factor_out(t) * dot_nn(writers, leaving)
        dx_send[:, :, cols] = result.astype(BF16).reshape(ny, rows, LANES)
        gw = gw + dot_nt(ev_ref[:, cols], jnp.concatenate([leaving, nothing], axis=0))
    gw_send[...] = gw.astype(BF16).reshape(ny, rows, LANES)
    each(ny - 1, lambda i: y_copy(6, i + 1, gw_send.at[y_peer(i + 1)], gw_recv.at[me]).start())
    each(ny - 1, lambda i: y_copy(5, i + 1, dx_send.at[y_peer(i + 1)], dx_ref.at[:, wide(me)]).start())
    own_dx = pltpu.make_async_copy(dx_send.at[me], dx_ref.at[:, wide(me)], own_sem.at[3])
    own_dx.start()
    gw_recv[me] = gw_send[me]

    def drain_y(i):
        k = i + 1
        y_copy(0, k, st_send, st_buf.at[me]).wait_send()
        y_copy(1, k, wr_send.at[y_peer(k)], wr_buf.at[me]).wait_send()
        y_copy(2, k, x_ref.at[:, wide(y_peer(k))], v_buf.at[me]).wait_send()
        y_copy(3, k, g_ref.at[:, wide(y_peer(k))], g_buf.at[me]).wait_send()

    def drain_z(i):
        k = i + 1
        z_copy(0, k, dec_send.at[0], dec_recv.at[zme]).wait_send()
        z_copy(1, k, f_send.at[z_peer(k)], f_recv.at[zme]).wait_send()
        z_copy(2, k, b_send.at[z_peer(k)], b_recv.at[zme]).wait_send()
        z_copy(3, k, rf_send.at[z_peer(k)], rf_recv.at[zme]).wait_send()
        z_copy(4, k, rb_send.at[z_peer(k)], rb_recv.at[zme]).wait_send()

    def drain_x(i):
        k = i + 1
        x_copy(0, k, xf_send, xf_recv.at[xme]).wait_send()
        x_copy(1, k, xb_send, xb_recv.at[xme]).wait_send()

    each(ny - 1, drain_y)
    each(nz - 1, drain_z)
    each(nx - 1, drain_x)

    each(ny - 1, lambda i: y_copy(6, i + 1, gw_send.at[y_peer(i + 1)], gw_recv.at[y_from(i + 1)]).wait_recv())
    low = lax.broadcasted_iota(jnp.int32, (rows, LANES), 1) < 64
    for pair in range(ny // 2):
        cols = slice(pair * LANES, (pair + 1) * LANES)
        even = gw_recv[2 * pair].astype(F32)
        odd = gw_recv[2 * pair + 1].astype(F32)
        dw_ref[:, cols] = jnp.where(low, even, pltpu.roll(odd, 64, 1)).astype(BF16)
        dr_ref[:, cols] = jnp.where(low, pltpu.roll(even, 64, 1), odd).astype(BF16)

    def finish(i):
        k = i + 1
        y_copy(4, k, out_send.at[y_peer(k)], out_ref.at[:, wide(y_from(k))]).wait()
        y_copy(5, k, dx_send.at[y_peer(k)], dx_ref.at[:, wide(y_from(k))]).wait()
        y_copy(6, k, gw_send.at[y_peer(k)], gw_recv.at[me]).wait_send()

    each(ny - 1, finish)
    own_out.wait()
    own_dx.wait()


def on_device(nx, nz, ny, inputs, step_sizes, decay_rates, state_write, state_read, doc_lengths, out_grad):
    rows = BLOCK // ny
    piece = STATE // (nz // PAIRS)
    vmem = pl.BlockSpec(memory_space=pltpu.VMEM)
    smem = pl.BlockSpec(memory_space=pltpu.SMEM)
    anywhere = pl.BlockSpec(memory_space=pl.ANY)
    wide_shape = jax.ShapeDtypeStruct(inputs.shape, BF16)
    thin_shape = jax.ShapeDtypeStruct(state_write.shape, BF16)
    bf = lambda *shape: pltpu.VMEM(shape, BF16)
    fl = lambda *shape: pltpu.VMEM(shape, F32)
    return pl.pallas_call(
        functools.partial(kernel, nx, nz, ny),
        out_shape=(wide_shape, wide_shape, thin_shape, thin_shape),
        in_specs=[anywhere, vmem, smem, vmem, vmem, smem, anywhere],
        out_specs=(anywhere, anywhere, vmem, vmem),
        scratch_shapes=[
            bf(rows, LANES), bf(ny, rows, LANES), bf(ny, rows, LANES), bf(ny, rows, LANES),
            bf(ny, rows, WIDE), bf(ny, rows, WIDE),
            fl(PAIRS, 1, LANES), fl(nz, 1, LANES),
            bf(nz, piece, LANES), bf(nz, piece, LANES), bf(nz, piece, LANES), bf(nz, piece, LANES),
            fl(piece + 8, LANES), fl(nx, piece + 8, LANES), fl(piece, LANES), fl(nx, piece, LANES),
            bf(nz, piece, LANES), bf(nz, piece, LANES), bf(nz, piece, LANES), bf(nz, piece, LANES),
            bf(ny, rows, WIDE), bf(ny, rows, WIDE), bf(ny, rows, LANES), bf(ny, rows, LANES),
            fl(BLOCK, HEADS_HERE * LANES), fl(HEADS_HERE, BLOCK), fl(BLOCK, BLOCK), fl(BLOCK, BLOCK),
            fl(BLOCK, BLOCK), bf(BLOCK, WIDE), bf(BLOCK, WIDE), fl(BLOCK, WIDE), fl(BLOCK, WIDE),
            pltpu.SemaphoreType.DMA((7, ny)), pltpu.SemaphoreType.DMA((7, ny)),
            pltpu.SemaphoreType.DMA((5, nz)), pltpu.SemaphoreType.DMA((5, nz)),
            pltpu.SemaphoreType.DMA((2, nx)), pltpu.SemaphoreType.DMA((2, nx)),
            pltpu.SemaphoreType.DMA((4,)),
        ],
        compiler_params=pltpu.CompilerParams(collective_id=0, has_side_effects=True),
    )(inputs, step_sizes, decay_rates, state_write, state_read, doc_lengths, out_grad)


def solution(mesh):
    nctx, ny = mesh.shape["ctx"], mesh.shape["head"]
    nz = 16 if nctx % 16 == 0 else nctx // 2
    nx = nctx // nz
    rows = P(("ctx", "head"), None)
    return jax.shard_map(
        functools.partial(on_device, nx, nz, ny),
        mesh=mesh,
        in_specs=(rows, rows, P("head"), rows, rows, P(), rows),
        out_specs=(rows, rows, rows, rows),
        check_vma=False,
    )
```

time: 550 us -> 61.3 us (0.11)
  waiting for transfers between devices: 228 us -> 0 us
  other arithmetic: 137 us -> 0 us
  blocking collectives: 67.2 us -> 0 us
  Pallas kernels: 0 us -> 56.5 us
  starting transfers between devices: 55.8 us -> 0 us
  local copies, waits for them, and re-layouts: 32 us -> 3.86 us
  between operations: 15.6 us -> 0.65 us
  matrix products: 5.53 us -> 0 us
    all_gather x2 -> x0, waiting for transfers between devices: 202 us -> none  [carried_in(): pieces = jax.tree.map(lambda part: lax.all_gather(part, axis), value)]
    select_n x126 -> x0, other arithmetic: 133 us -> none  [turn(): jnp.where(position < mine, new, old)]
    all_gather x1 -> x0, blocking collectives: 67.2 us -> none  [carried_in(): pieces = jax.tree.map(lambda part: lax.all_gather(part, axis), value)]
    pallas_call x0 -> x1, Pallas kernels: none -> 56.5 us  [on_device(): pl.pallas_call(functools.partial(kernel, nx, nz, ny), out_shape=(wide_sha...]
    all_to_all x9 -> x0, starting transfers between devices: 55.8 us -> none  [the longest x1 13.4 us: on_device(): lax.all_to_all(inputs, 'head', split_axis=1, concat_axis=0, tiled=True)]
    all_to_all x9 -> x0, waiting for transfers between devices: 26.7 us -> none  [the longest x1 6.21 us: on_device(): lax.all_to_all(out_grad, 'head', split_axis=1, concat_axis=0, tiled=True)]
    rev x2 -> x0, local copies, waits for them, and re-layouts: 11.8 us -> none  [carried_in(): pieces = jax.tree.map(lambda part: part[::-1], pieces)]
    all_to_all x14 -> x0, local copies, waits for them, and re-layouts: 8.42 us -> none  [the longest x2 1.75 us: on_device(): lax.all_to_all(result, 'head', split_axis=0, concat_axis=1, tiled=True)]
  transfers between devices with their start and end apart: 11 -> 0, of which waited for: 8 -> 0; matrix products, arithmetic and copies ran while one was open for 30% -> 0% of each run, Pallas kernels for 0% -> 0%
where the time goes in v1:
time: 61.3 us; the launch traced here: 61 us
  Pallas kernels  56.5 us (92%)
  local copies, waits for them, and re-layouts  3.86 us (6%)
  between operations  0.65 us (1%)
    pallas_call x1, Pallas kernels, on_device(): pl.pallas_call(functools.partial(kernel, nx, nz, ny), out_shape=(wide_sha...  56.5 us
    unnamed x10, local copies, waits for them, and re-layouts  3.86 us

profile of v1, /device:TPU:1, one launch (start us, length us, event | category | flops | bytes accessed | tf_op | source)
XLA Modules:
  0.0 61.0 jit_solution(15646547632536674457)
XLA Ops:
  0.6 56.5 %shard_map.102 = (bf16[32,4096]{1,0:T(8,128)(2,1)}, bf16[32,4096]{1,0:T(8,128)(2,1)}, bf16[32,512]{1,0:T(8,128)(2,1)}, bf16[32,512]{1,0:T(8,128)(2,1)}) custom-call(bf16[32,4096]{1,0:T(8,128)(2,1)} %x_ref.1, bf16[32,64]{1,0:T(8,128)(2,1)} %step_ref.1, f32[8]{0:T(128)} %rate_ref.1, bf16[32,512]{1,0:T(8,128)(2,1)} %w_ref.1, bf16[32,512]{1,0:T(8,128)(2,1)} %r_ref.1, ...), custom_call_target="tpu_custom_call" | custom-call | tf_op jit(solution)/shard_map/pallas_call | solution.py:405
  57.1 0.0 copy-start
  57.1 1.7 %copy.15 = bf16[32,4096]{1,0:T(8,128)(2,1)} copy(bf16[32,4096]{1,0:T(8,128)(2,1)} %get-tuple-element.8) | data formatting | bytes 524288
  58.8 0.0 copy-done
  58.8 0.0 copy-start.2
  58.8 0.7 %copy.16 = bf16[32,4096]{1,0:T(8,128)(2,1)} copy(bf16[32,4096]{1,0:T(8,128)(2,1)S(1)} %copy-done) | data formatting | bytes 524288
  59.5 0.1 copy-done.2
  59.6 0.0 copy-start.1
  59.6 0.6 %copy.17 = bf16[32,512]{1,0:T(8,128)(2,1)} copy(bf16[32,512]{1,0:T(8,128)(2,1)S(1)} %copy-done.2) | data formatting | bytes 65536
  60.2 0.2 copy-done.1
  60.4 0.6 %copy.18 = bf16[32,512]{1,0:T(8,128)(2,1)} copy(bf16[32,512]{1,0:T(8,128)(2,1)S(1)} %copy-done.1) | data formatting | bytes 65536
Async XLA Ops:
  57.1 1.7 %copy-start = (bf16[32,4096]{1,0:T(8,128)(2,1)S(1)}, bf16[32,4096]{1,0:T(8,128)(2,1)}, u32[]{:S(2)}) copy-start(bf16[32,4096]{1,0:T(8,128)(2,1)} %get-tuple-element.9) | copy-start | bytes 786436
  58.8 0.8 %copy-start.2 = (bf16[32,512]{1,0:T(8,128)(2,1)S(1)}, bf16[32,512]{1,0:T(8,128)(2,1)}, u32[]{:S(2)}) copy-start(bf16[32,512]{1,0:T(8,128)(2,1)} %get-tuple-element.10) | copy-start | bytes 98308
  59.6 0.8 %copy-start.1 = (bf16[32,512]{1,0:T(8,128)(2,1)S(1)}, bf16[32,512]{1,0:T(8,128)(2,1)}, u32[]{:S(2)}) copy-start(bf16[32,512]{1,0:T(8,128)(2,1)} %get-tuple-element.11) | copy-start | bytes 98308

commit v2 on v1

--- a/solution.py
+++ b/solution.py
@@ -35,14 +35,15 @@
 def kernel(
     nx, nz, ny,
     x_ref, step_ref, rate_ref, w_ref, r_ref, doc_ref, g_ref,
-    out_ref, dx_ref, dw_ref, dr_ref,
+    out_ref, dx_ref, gw_recv,
+    x_in, g_in, step_in, w_in, r_in, rate_in, doc_in,
     st_send, st_buf, wr_send, wr_buf, v_buf, g_buf,
     dec_send, dec_recv, f_send, f_recv, b_send, b_recv,
     xf_send, xf_recv, xb_send, xb_recv,
     rf_send, rf_recv, rb_send, rb_recv,
-    out_send, dx_send, gw_send, gw_recv,
+    out_send, dx_send, gw_send,
     run_col, run_row, bias_ref, score_ref, dscore_ref, ev_ref, cg_ref, loc_ref, dv_ref,
-    y_ssem, y_rsem, z_ssem, z_rsem, x_ssem, x_rsem, own_sem,
+    y_ssem, y_rsem, z_ssem, z_rsem, x_ssem, x_rsem, own_sem, ready,
 ):
     rows = BLOCK // ny
     blocks_of = nz // PAIRS
@@ -86,6 +87,18 @@
             src_ref=src, dst_ref=dst, send_sem=x_ssem.at[cat, k], recv_sem=x_rsem.at[cat, k],
             device_id={"ctx": x_peer(k) * nz + zme, "head": me}, device_id_type=pl.DeviceIdType.MESH)
 
+    def signal_y(sem, k):
+        pl.semaphore_signal(
+            sem, inc=1, device_id={"ctx": ctx, "head": y_peer(k)}, device_id_type=pl.DeviceIdType.MESH)
+
+    def signal_z(sem, k):
+        pl.semaphore_signal(
+            sem, inc=1, device_id={"ctx": base + z_peer(k), "head": me}, device_id_type=pl.DeviceIdType.MESH)
+
+    def signal_x(sem, k):
+        pl.semaphore_signal(
+            sem, inc=1, device_id={"ctx": x_peer(k) * nz + zme, "head": me}, device_id_type=pl.DeviceIdType.MESH)
+
     def wide(at):
         return pl.ds(pl.multiple_of(at * WIDE, WIDE), WIDE)
 
@@ -101,34 +114,73 @@
         lax.fori_loop(0, count, step, 0)
 
     barrier = pltpu.get_barrier_semaphore()
-    each(ny - 1, lambda i: pl.semaphore_signal(
-        barrier, inc=1, device_id={"ctx": ctx, "head": y_peer(i + 1)}, device_id_type=pl.DeviceIdType.MESH))
-    each(nx - 1, lambda i: pl.semaphore_signal(
-        barrier, inc=1, device_id={"ctx": x_peer(i + 1) * nz + zme, "head": me}, device_id_type=pl.DeviceIdType.MESH))
-    each(nz - 1, lambda i: pl.semaphore_signal(
-        barrier, inc=1, device_id={"ctx": base + z_peer(i + 1), "head": me}, device_id_type=pl.DeviceIdType.MESH))
-
-    own_v = pltpu.make_async_copy(x_ref.at[:, wide(me)], v_buf.at[me], own_sem.at[0])
-    own_g = pltpu.make_async_copy(g_ref.at[:, wide(me)], g_buf.at[me], own_sem.at[1])
-    own_v.start()
-    own_g.start()
+    x_near = sorted({1, nx - 1})
+    each(ny - 1, lambda i: signal_y(barrier, i + 1))
+    for k in x_near:
+        signal_x(barrier, k)
+    for k in (1, nz - 1):
+        signal_z(barrier, k)
+
+    fetch = [
+        pltpu.make_async_copy(src, dst, own_sem.at[i])
+        for i, (src, dst) in enumerate((
+            (step_ref, step_in), (w_ref, w_in), (r_ref, r_in), (x_ref, x_in), (g_ref, g_in),
+            (doc_ref, doc_in), (rate_ref, rate_in)))
+    ]
+    for copy in fetch:
+        copy.start()
+
     low = lax.broadcasted_iota(jnp.int32, (rows, LANES), 1) < 64
     st_send[...] = jnp.zeros((rows, LANES), BF16)
-    st_send[:, 0:ny * HEADS_HERE] = step_ref[...]
+    for copy in fetch[0:3]:
+        copy.wait()
+    st_send[:, 0:ny * HEADS_HERE] = step_in[...]
     for pair in range(ny // 2):
         cols = slice(pair * LANES, (pair + 1) * LANES)
-        w2 = w_ref[:, cols].astype(F32)
-        r2 = r_ref[:, cols].astype(F32)
+        w2 = w_in[:, cols].astype(F32)
+        r2 = r_in[:, cols].astype(F32)
         wr_send[2 * pair] = jnp.where(low, w2, pltpu.roll(r2, 64, 1)).astype(BF16)
         wr_send[2 * pair + 1] = jnp.where(low, pltpu.roll(w2, 64, 1), r2).astype(BF16)
+    fetch[3].wait()
+    fetch[4].wait()
+    pl.semaphore_wait(barrier, ny - 1 + len(x_near) + 2)
+
+    def send_small(i):
+        y_copy(0, i + 1, st_send, st_buf.at[me]).start()
+        y_copy(1, i + 1, wr_send.at[y_peer(i + 1)], wr_buf.at[me]).start()
+
+    each(ny - 1, send_small)
+    each(ny - 1, lambda i: y_copy(2, i + 1, x_in.at[:, wide(y_peer(i + 1))], v_buf.at[me]).start())
+    each(ny - 1, lambda i: y_copy(3, i + 1, g_in.at[:, wide(y_peer(i + 1))], g_buf.at[me]).start())
+
+    steps_z = []
+    radius = 1
+    while radius < nz // 2:
+        steps_z.append(radius)
+        radius *= 2
+
+    def reach_start(at):
+        for k in (steps_z[at], nz - steps_z[at]):
+            signal_z(ready.at[at], k)
+
+    def reach_end(at):
+        pl.semaphore_wait(ready.at[at], 2)
+
+    reach_start(0)
+    if nx > 2:
+        signal_x(ready.at[3], 1)
+        signal_x(ready.at[3], nx - 1)
+    v_buf[me] = x_in[:, wide(me)]
+    g_buf[me] = g_in[:, wide(me)]
     st_buf[me] = st_send[...]
     wr_buf[me] = wr_send[me]
-
+    fetch[5].wait()
+    fetch[6].wait()
     first = ctx * BLOCK
     starts, at = [], jnp.int32(0)
     for k in range(DOCS):
         starts.append(at)
-        at = at + doc_ref[k]
+        at = at + doc_in[k]
 
     def segment(pos):
         seg = jnp.where(starts[0] <= pos, 1, 0)
@@ -138,6 +190,9 @@
 
     seg_before = segment(first - 1)
     seg_last = segment(first + BLOCK - 1)
+    reach_end(0)
+    if len(steps_z) > 1:
+        reach_start(1)
     seg_col = segment(first + lax.broadcasted_iota(jnp.int32, (BLOCK, LANES), 0))
     seg_row = segment(first + lax.broadcasted_iota(jnp.int32, (8, BLOCK), 1))[0:1]
     row_i = lax.broadcasted_iota(jnp.int32, (BLOCK, BLOCK), 0)
@@ -145,16 +200,14 @@
     causal = row_i >= col_i
     seg_wide = jnp.concatenate([seg_col, seg_col], axis=1)
     bias_ref[...] = jnp.where(causal & (seg_wide == seg_row), 0.0, NEG)
+    dscore_ref[...] = jnp.zeros((BLOCK, BLOCK), F32)
     through = jnp.where(seg_last == seg_before, 1.0, 0.0)
-    pl.semaphore_wait(barrier, ny - 1 + nz - 1 + nx - 1)
-
-    def send_small(i):
-        y_copy(0, i + 1, st_send, st_buf.at[me]).start()
-        y_copy(1, i + 1, wr_send.at[y_peer(i + 1)], wr_buf.at[me]).start()
-
-    each(ny - 1, send_small)
-    each(ny - 1, lambda i: y_copy(2, i + 1, x_ref.at[:, wide(y_peer(i + 1))], v_buf.at[me]).start())
-    each(ny - 1, lambda i: y_copy(3, i + 1, g_ref.at[:, wide(y_peer(i + 1))], g_buf.at[me]).start())
+    if nx > 2:
+        pl.semaphore_wait(ready.at[3], 2)
+    if len(steps_z) > 1:
+        reach_end(1)
+    if len(steps_z) > 2:
+        reach_start(2)
 
     each(ny - 1, lambda i: y_copy(0, i + 1, st_send, st_buf.at[y_from(i + 1)]).wait_recv())
     steps = st_buf[...].reshape(BLOCK, LANES)
@@ -167,8 +220,8 @@
     steps_row = dot_nt(jnp.where(pick_row, 1.0, 0.0).astype(BF16), steps).astype(BF16)
     summed_row = dot_nn(steps_row, jnp.where(row_i <= col_i, 1.0, 0.0).astype(BF16))
     for h in range(HEADS_HERE):
-        run_col[:, h * LANES:(h + 1) * LANES] = summed[:, h * LANES:(h + 1) * LANES] * (-rate_ref[h])
-        run_row[h:h + 1, :] = summed_row[h:h + 1, :] * (-rate_ref[h])
+        run_col[:, h * LANES:(h + 1) * LANES] = summed[:, h * LANES:(h + 1) * LANES] * (-rate_in[h])
+        run_row[h:h + 1, :] = summed_row[h:h + 1, :] * (-rate_in[h])
     low = lax.broadcasted_iota(jnp.int32, (BLOCK, LANES), 1) < 64
     low_row = low[0:1]
 
@@ -194,6 +247,8 @@
         k = z_offset(i)
         z_copy(0, k, dec_send.at[lax.div(z_peer(k), blocks_of)], dec_recv.at[zme]).start()
 
+    if len(steps_z) > 2:
+        reach_end(2)
     each(nz - 1, send_decay)
 
     each(ny - 1, lambda i: y_copy(1, i + 1, wr_send.at[y_peer(i + 1)], wr_buf.at[y_from(i + 1)]).wait_recv())
@@ -205,8 +260,7 @@
     write_high = jnp.where(low, 0.0, rw).astype(BF16)
     score_ref[...] = dot_nt(readers, writers)
 
-    own_v.wait()
-    each(ny - 1, lambda i: y_copy(2, i + 1, x_ref.at[:, wide(y_peer(i + 1))], v_buf.at[y_from(i + 1)]).wait_recv())
+    each(ny - 1, lambda i: y_copy(2, i + 1, x_in.at[:, wide(y_peer(i + 1))], v_buf.at[y_from(i + 1)]).wait_recv())
     for t in range(PAIRS):
         cols = slice(t * LANES, (t + 1) * LANES)
         values = v_buf[:, :, cols].reshape(BLOCK, LANES)
@@ -222,8 +276,7 @@
     each(nz - 1, send_f)
     f_recv[zme] = f_send[zme]
 
-    own_g.wait()
-    each(ny - 1, lambda i: y_copy(3, i + 1, g_ref.at[:, wide(y_peer(i + 1))], g_buf.at[y_from(i + 1)]).wait_recv())
+    each(ny - 1, lambda i: y_copy(3, i + 1, g_in.at[:, wide(y_peer(i + 1))], g_buf.at[y_from(i + 1)]).wait_recv())
     for t in range(PAIRS):
         cols = slice(t * LANES, (t + 1) * LANES)
         grads = g_buf[:, :, cols].reshape(BLOCK, LANES)
@@ -239,7 +292,6 @@
     each(nz - 1, send_b)
     b_recv[zme] = b_send[zme]
 
-    dscore_ref[...] = jnp.zeros((BLOCK, BLOCK), F32)
     low_one = jnp.where(low_row, 1.0, 0.0).astype(BF16)
     high_one = jnp.where(low_row, 0.0, 1.0).astype(BF16)
 
@@ -331,8 +383,7 @@
         out_send[:, :, cols] = result.astype(BF16).reshape(ny, rows, LANES)
         gw = gw + dot_nt(cg_ref[:, cols], jnp.concatenate([nothing, entering], axis=0))
     each(ny - 1, lambda i: y_copy(4, i + 1, out_send.at[y_peer(i + 1)], out_ref.at[:, wide(me)]).start())
-    own_out = pltpu.make_async_copy(out_send.at[me], out_ref.at[:, wide(me)], own_sem.at[2])
-    own_out.start()
+    out_ref[:, wide(me)] = out_send[me]
 
     each(nz - 1, lambda i: z_copy(4, i + 1, rb_send.at[0], rb_recv.at[z_from(i + 1)]).wait_recv())
     for t in range(PAIRS):
@@ -344,16 +395,15 @@
     gw_send[...] = gw.astype(BF16).reshape(ny, rows, LANES)
     each(ny - 1, lambda i: y_copy(6, i + 1, gw_send.at[y_peer(i + 1)], gw_recv.at[me]).start())
     each(ny - 1, lambda i: y_copy(5, i + 1, dx_send.at[y_peer(i + 1)], dx_ref.at[:, wide(me)]).start())
-    own_dx = pltpu.make_async_copy(dx_send.at[me], dx_ref.at[:, wide(me)], own_sem.at[3])
-    own_dx.start()
+    dx_ref[:, wide(me)] = dx_send[me]
     gw_recv[me] = gw_send[me]
 
     def drain_y(i):
         k = i + 1
         y_copy(0, k, st_send, st_buf.at[me]).wait_send()
         y_copy(1, k, wr_send.at[y_peer(k)], wr_buf.at[me]).wait_send()
-        y_copy(2, k, x_ref.at[:, wide(y_peer(k))], v_buf.at[me]).wait_send()
-        y_copy(3, k, g_ref.at[:, wide(y_peer(k))], g_buf.at[me]).wait_send()
+        y_copy(2, k, x_in.at[:, wide(y_peer(k))], v_buf.at[me]).wait_send()
+        y_copy(3, k, g_in.at[:, wide(y_peer(k))], g_buf.at[me]).wait_send()
 
     def drain_z(i):
         k = i + 1
@@ -372,58 +422,78 @@
     each(nz - 1, drain_z)
     each(nx - 1, drain_x)
 
-    each(ny - 1, lambda i: y_copy(6, i + 1, gw_send.at[y_peer(i + 1)], gw_recv.at[y_from(i + 1)]).wait_recv())
+    def finish(i):
+        k = i + 1
+        y_copy(4, k, out_send.at[y_peer(k)], out_ref.at[:, wide(y_from(k))]).wait()
+        y_copy(6, k, gw_send.at[y_peer(k)], gw_recv.at[y_from(k)]).wait()
+        y_copy(5, k, dx_send.at[y_peer(k)], dx_ref.at[:, wide(y_from(k))]).wait()
+
+    each(ny - 1, finish)
+
+
+def last(ny, out_in, dx_in, gw_in, out_ref, dx_ref, dw_ref, dr_ref, dw_out, dr_out, sem):
+    rows = BLOCK // ny
+    out_copy = pltpu.make_async_copy(out_in, out_ref, sem.at[0])
+    dx_copy = pltpu.make_async_copy(dx_in, dx_ref, sem.at[1])
+    dw_copy = pltpu.make_async_copy(dw_out, dw_ref, sem.at[2])
+    dr_copy = pltpu.make_async_copy(dr_out, dr_ref, sem.at[3])
+    out_copy.start()
+    dx_copy.start()
     low = lax.broadcasted_iota(jnp.int32, (rows, LANES), 1) < 64
     for pair in range(ny // 2):
         cols = slice(pair * LANES, (pair + 1) * LANES)
-        even = gw_recv[2 * pair].astype(F32)
-        odd = gw_recv[2 * pair + 1].astype(F32)
-        dw_ref[:, cols] = jnp.where(low, even, pltpu.roll(odd, 64, 1)).astype(BF16)
-        dr_ref[:, cols] = jnp.where(low, pltpu.roll(even, 64, 1), odd).astype(BF16)
-
-    def finish(i):
-        k = i + 1
-        y_copy(4, k, out_send.at[y_peer(k)], out_ref.at[:, wide(y_from(k))]).wait()
-        y_copy(5, k, dx_send.at[y_peer(k)], dx_ref.at[:, wide(y_from(k))]).wait()
-        y_copy(6, k, gw_send.at[y_peer(k)], gw_recv.at[me]).wait_send()
-
-    each(ny - 1, finish)
-    own_out.wait()
-    own_dx.wait()
+        even = gw_in[2 * pair].astype(F32)
+        odd = gw_in[2 * pair + 1].astype(F32)
+        dw_out[:, cols] = jnp.where(low, even, pltpu.roll(odd, 64, 1)).astype(BF16)
+        dr_out[:, cols] = jnp.where(low, pltpu.roll(even, 64, 1), odd).astype(BF16)
+    dw_copy.start()
+    dr_copy.start()
+    out_copy.wait()
+    dx_copy.wait()
+    dw_copy.wait()
+    dr_copy.wait()
 
 
 def on_device(nx, nz, ny, inputs, step_sizes, decay_rates, state_write, state_read, doc_lengths, out_grad):
     rows = BLOCK // ny
     piece = STATE // (nz // PAIRS)
     vmem = pl.BlockSpec(memory_space=pltpu.VMEM)
-    smem = pl.BlockSpec(memory_space=pltpu.SMEM)
     anywhere = pl.BlockSpec(memory_space=pl.ANY)
     wide_shape = jax.ShapeDtypeStruct(inputs.shape, BF16)
     thin_shape = jax.ShapeDtypeStruct(state_write.shape, BF16)
     bf = lambda *shape: pltpu.VMEM(shape, BF16)
     fl = lambda *shape: pltpu.VMEM(shape, F32)
-    return pl.pallas_call(
+    outs = pl.pallas_call(
         functools.partial(kernel, nx, nz, ny),
-        out_shape=(wide_shape, wide_shape, thin_shape, thin_shape),
-        in_specs=[anywhere, vmem, smem, vmem, vmem, smem, anywhere],
-        out_specs=(anywhere, anywhere, vmem, vmem),
+        out_shape=(bf(*inputs.shape), bf(*inputs.shape), bf(ny, rows, LANES)),
+        in_specs=[anywhere] * 7,
+        out_specs=(vmem, vmem, vmem),
         scratch_shapes=[
+            bf(rows, ny * WIDE), bf(rows, ny * WIDE), bf(*step_sizes.shape), bf(*state_write.shape),
+            bf(*state_read.shape), pltpu.SMEM(decay_rates.shape, F32), pltpu.SMEM((DOCS,), jnp.int32),
             bf(rows, LANES), bf(ny, rows, LANES), bf(ny, rows, LANES), bf(ny, rows, LANES),
             bf(ny, rows, WIDE), bf(ny, rows, WIDE),
             fl(PAIRS, 1, LANES), fl(nz, 1, LANES),
             bf(nz, piece, LANES), bf(nz, piece, LANES), bf(nz, piece, LANES), bf(nz, piece, LANES),
             fl(piece + 8, LANES), fl(nx, piece + 8, LANES), fl(piece, LANES), fl(nx, piece, LANES),
             bf(nz, piece, LANES), bf(nz, piece, LANES), bf(nz, piece, LANES), bf(nz, piece, LANES),
-            bf(ny, rows, WIDE), bf(ny, rows, WIDE), bf(ny, rows, LANES), bf(ny, rows, LANES),
+            bf(ny, rows, WIDE), bf(ny, rows, WIDE), bf(ny, rows, LANES),
             fl(BLOCK, HEADS_HERE * LANES), fl(HEADS_HERE, BLOCK), fl(BLOCK, BLOCK), fl(BLOCK, BLOCK),
             fl(BLOCK, BLOCK), bf(BLOCK, WIDE), bf(BLOCK, WIDE), fl(BLOCK, WIDE), fl(BLOCK, WIDE),
             pltpu.SemaphoreType.DMA((7, ny)), pltpu.SemaphoreType.DMA((7, ny)),
             pltpu.SemaphoreType.DMA((5, nz)), pltpu.SemaphoreType.DMA((5, nz)),
             pltpu.SemaphoreType.DMA((2, nx)), pltpu.SemaphoreType.DMA((2, nx)),
-            pltpu.SemaphoreType.DMA((4,)),
+            pltpu.SemaphoreType.DMA((7,)), pltpu.SemaphoreType.REGULAR((4,)),
         ],
         compiler_params=pltpu.CompilerParams(collective_id=0, has_side_effects=True),
     )(inputs, step_sizes, decay_rates, state_write, state_read, doc_lengths, out_grad)
+    return pl.pallas_call(
+        functools.partial(last, ny),
+        out_shape=(wide_shape, wide_shape, thin_shape, thin_shape),
+        in_specs=[vmem, vmem, vmem],
+        out_specs=(anywhere, anywhere, anywhere, anywhere),
+        scratch_shapes=[bf(*state_write.shape), bf(*state_read.shape), pltpu.SemaphoreType.DMA((4,))],
+    )(*[pltpu.with_memory_space_constraint(part, pltpu.VMEM) for part in outs])
 
 
 def solution(mesh):

time: 61.3 us -> 52.1 us (0.85)
  Pallas kernels: 56.5 us -> 51.4 us
  local copies, waits for them, and re-layouts: 3.86 us -> 0 us
    pallas_call x1 -> x2, Pallas kernels: 56.5 us -> 51.4 us  [the longest x1 50.5 us: on_device(): pl.pallas_call(functools.partial(kernel, nx, nz, ny), out_shape=(bf(*inpu...]
    unnamed x10 -> x0, local copies, waits for them, and re-layouts: 3.86 us -> none
where the time goes in v2:
time: 52.1 us; the launch traced here: 52 us
  Pallas kernels  51.4 us (99%)
  between operations  0.64 us (1%)
    pallas_call x1, Pallas kernels, on_device(): pl.pallas_call(functools.partial(kernel, nx, nz, ny), out_shape=(bf(*inpu...  50.5 us

profile of v2, /device:TPU:1, one launch (start us, length us, event | category | flops | bytes accessed | tf_op | source)
XLA Modules:
  0.0 52.0 jit_solution(4761717380742818373)
XLA Ops:
  0.6 50.5 %shard_map.102 = (bf16[32,4096]{1,0:T(8,128)(2,1)S(1)}, bf16[32,4096]{1,0:T(8,128)(2,1)S(1)}, bf16[8,32,128]{2,1,0:T(8,128)(2,1)S(1)}) custom-call(bf16[32,4096]{1,0:T(8,128)(2,1)} %x_ref.1, bf16[32,64]{1,0:T(8,128)(2,1)} %step_ref.1, f32[8]{0:T(128)} %rate_ref.1, bf16[32,512]{1,0:T(8,128)(2,1)} %w_ref.1, bf16[32,512]{1,0:T(8,128)(2,1)} %r_ref.1, ...), custom_call_target="tpu_custom_call" | custom-call | tf_op jit(solution)/shard_map/pallas_call | solution.py:466
  51.2 0.8 %shard_map.103 = (bf16[32,4096]{1,0:T(8,128)(2,1)}, bf16[32,4096]{1,0:T(8,128)(2,1)}, bf16[32,512]{1,0:T(8,128)(2,1)}, bf16[32,512]{1,0:T(8,128)(2,1)}) custom-call(bf16[32,4096]{1,0:T(8,128)(2,1)S(1)} %get-tuple-element.7.out_in, bf16[32,4096]{1,0:T(8,128)(2,1)S(1)} %get-tuple-element.8.dx_in, bf16[8,32,128]{2,1,0:T(8,128)(2,1)S(1)} %get-tuple-element.9.gw_in), custom_call_target="tpu_custom_call" | custom-call | tf_op jit(solution)/shard_map/pallas_call | solution.py:490

commit v3 on v2

--- a/solution.py
+++ b/solution.py
@@ -37,12 +37,12 @@
     x_ref, step_ref, rate_ref, w_ref, r_ref, doc_ref, g_ref,
     out_ref, dx_ref, gw_recv,
     x_in, g_in, step_in, w_in, r_in, rate_in, doc_in,
-    st_send, st_buf, wr_send, wr_buf, v_buf, g_buf,
+    sw_send, sw_buf, v_buf, g_buf,
     dec_send, dec_recv, f_send, f_recv, b_send, b_recv,
     xf_send, xf_recv, xb_send, xb_recv,
     rf_send, rf_recv, rb_send, rb_recv,
     out_send, dx_send, gw_send,
-    run_col, run_row, bias_ref, score_ref, dscore_ref, ev_ref, cg_ref, loc_ref, dv_ref,
+    run_col, run_row, bias_ref, score_ref, dscore_ref, ev_ref, cg_ref, loc_ref, dv_ref, fin_ref, fout_ref,
     y_ssem, y_rsem, z_ssem, z_rsem, x_ssem, x_rsem, own_sem, ready,
 ):
     rows = BLOCK // ny
@@ -57,34 +57,25 @@
     def y_peer(k):
         return lax.rem(me + k, ny)
 
-    def y_from(k):
-        return lax.rem(me + ny - k, ny)
-
     def z_peer(k):
         return lax.rem(zme + k, nz)
 
-    def z_from(k):
-        return lax.rem(zme + nz - k, nz)
-
     def x_peer(k):
         return lax.rem(xme + k, nx)
 
-    def x_from(k):
-        return lax.rem(xme + nx - k, nx)
-
     def y_copy(cat, k, src, dst):
         return pltpu.make_async_remote_copy(
-            src_ref=src, dst_ref=dst, send_sem=y_ssem.at[cat, k], recv_sem=y_rsem.at[cat, k],
+            src_ref=src, dst_ref=dst, send_sem=y_ssem.at[cat], recv_sem=y_rsem.at[cat],
             device_id={"ctx": ctx, "head": y_peer(k)}, device_id_type=pl.DeviceIdType.MESH)
 
     def z_copy(cat, k, src, dst):
         return pltpu.make_async_remote_copy(
-            src_ref=src, dst_ref=dst, send_sem=z_ssem.at[cat, k], recv_sem=z_rsem.at[cat, k],
+            src_ref=src, dst_ref=dst, send_sem=z_ssem.at[cat], recv_sem=z_rsem.at[cat],
             device_id={"ctx": base + z_peer(k), "head": me}, device_id_type=pl.DeviceIdType.MESH)
 
     def x_copy(cat, k, src, dst):
         return pltpu.make_async_remote_copy(
-            src_ref=src, dst_ref=dst, send_sem=x_ssem.at[cat, k], recv_sem=x_rsem.at[cat, k],
+            src_ref=src, dst_ref=dst, send_sem=x_ssem.at[cat], recv_sem=x_rsem.at[cat],
             device_id={"ctx": x_peer(k) * nz + zme, "head": me}, device_id_type=pl.DeviceIdType.MESH)
 
     def signal_y(sem, k):
@@ -102,20 +93,19 @@
     def wide(at):
         return pl.ds(pl.multiple_of(at * WIDE, WIDE), WIDE)
 
-    def z_offset(i):
-        half = lax.div(i + 1, 2)
-        return nz // 2 + half * (1 - 2 * lax.rem(i, 2))
-
-    def each(count, body):
-        def step(i, carry):
-            body(i)
-            return carry
-
-        lax.fori_loop(0, count, step, 0)
+    def far_first(n):
+        return sorted(range(1, n), key=lambda k: (-min(k, n - k), k))
+
+    def some(ref, n):
+        return ref.at[pl.ds(0, n - 1)]
+
+    def some_wide(ref):
+        return ref.at[:, pl.ds(0, (ny - 1) * WIDE)]
 
     barrier = pltpu.get_barrier_semaphore()
     x_near = sorted({1, nx - 1})
-    each(ny - 1, lambda i: signal_y(barrier, i + 1))
+    for k in far_first(ny):
+        signal_y(barrier, k)
     for k in x_near:
         signal_x(barrier, k)
     for k in (1, nz - 1):
@@ -131,27 +121,21 @@
         copy.start()
 
     low = lax.broadcasted_iota(jnp.int32, (rows, LANES), 1) < 64
-    st_send[...] = jnp.zeros((rows, LANES), BF16)
     for copy in fetch[0:3]:
         copy.wait()
-    st_send[:, 0:ny * HEADS_HERE] = step_in[...]
+    steps_here = step_in[...]
+    if ny * HEADS_HERE < LANES:
+        steps_here = jnp.concatenate([steps_here, jnp.zeros((rows, LANES - ny * HEADS_HERE), BF16)], axis=1)
     for pair in range(ny // 2):
         cols = slice(pair * LANES, (pair + 1) * LANES)
         w2 = w_in[:, cols].astype(F32)
         r2 = r_in[:, cols].astype(F32)
-        wr_send[2 * pair] = jnp.where(low, w2, pltpu.roll(r2, 64, 1)).astype(BF16)
-        wr_send[2 * pair + 1] = jnp.where(low, pltpu.roll(w2, 64, 1), r2).astype(BF16)
+        sw_send[2 * pair, :, 0:LANES] = steps_here
+        sw_send[2 * pair + 1, :, 0:LANES] = steps_here
+        sw_send[2 * pair, :, LANES:2 * LANES] = jnp.where(low, w2, pltpu.roll(r2, 64, 1)).astype(BF16)
+        sw_send[2 * pair + 1, :, LANES:2 * LANES] = jnp.where(low, pltpu.roll(w2, 64, 1), r2).astype(BF16)
     fetch[3].wait()
-    fetch[4].wait()
     pl.semaphore_wait(barrier, ny - 1 + len(x_near) + 2)
-
-    def send_small(i):
-        y_copy(0, i + 1, st_send, st_buf.at[me]).start()
-        y_copy(1, i + 1, wr_send.at[y_peer(i + 1)], wr_buf.at[me]).start()
-
-    each(ny - 1, send_small)
-    each(ny - 1, lambda i: y_copy(2, i + 1, x_in.at[:, wide(y_peer(i + 1))], v_buf.at[me]).start())
-    each(ny - 1, lambda i: y_copy(3, i + 1, g_in.at[:, wide(y_peer(i + 1))], g_buf.at[me]).start())
 
     steps_z = []
     radius = 1
@@ -160,20 +144,29 @@
         radius *= 2
 
     def reach_start(at):
-        for k in (steps_z[at], nz - steps_z[at]):
-            signal_z(ready.at[at], k)
+        if at < len(steps_z):
+            for k in (steps_z[at], nz - steps_z[at]):
+                signal_z(ready.at[at], k)
 
     def reach_end(at):
-        pl.semaphore_wait(ready.at[at], 2)
+        if at < len(steps_z):
+            pl.semaphore_wait(ready.at[at], 2)
 
     reach_start(0)
     if nx > 2:
         signal_x(ready.at[3], 1)
         signal_x(ready.at[3], nx - 1)
-    v_buf[me] = x_in[:, wide(me)]
-    g_buf[me] = g_in[:, wide(me)]
-    st_buf[me] = st_send[...]
-    wr_buf[me] = wr_send[me]
+
+    for k in far_first(ny):
+        y_copy(0, k, sw_send.at[y_peer(k)], sw_buf.at[me]).start()
+    for k in far_first(ny):
+        y_copy(1, k, x_in.at[:, wide(y_peer(k))], v_buf.at[me]).start()
+    reach_end(0)
+    reach_start(1)
+    fetch[4].wait()
+    for k in far_first(ny):
+        y_copy(2, k, g_in.at[:, wide(y_peer(k))], g_buf.at[me]).start()
+
     fetch[5].wait()
     fetch[6].wait()
     first = ctx * BLOCK
@@ -190,11 +183,15 @@
 
     seg_before = segment(first - 1)
     seg_last = segment(first + BLOCK - 1)
-    reach_end(0)
-    if len(steps_z) > 1:
-        reach_start(1)
     seg_col = segment(first + lax.broadcasted_iota(jnp.int32, (BLOCK, LANES), 0))
     seg_row = segment(first + lax.broadcasted_iota(jnp.int32, (8, BLOCK), 1))[0:1]
+    if nx > 2:
+        pl.semaphore_wait(ready.at[3], 2)
+    reach_end(1)
+    reach_start(2)
+    v_buf[me] = x_in[:, wide(me)]
+    g_buf[me] = g_in[:, wide(me)]
+    sw_buf[me] = sw_send[me]
     row_i = lax.broadcasted_iota(jnp.int32, (BLOCK, BLOCK), 0)
     col_i = lax.broadcasted_iota(jnp.int32, (BLOCK, BLOCK), 1)
     causal = row_i >= col_i
@@ -202,15 +199,10 @@
     bias_ref[...] = jnp.where(causal & (seg_wide == seg_row), 0.0, NEG)
     dscore_ref[...] = jnp.zeros((BLOCK, BLOCK), F32)
     through = jnp.where(seg_last == seg_before, 1.0, 0.0)
-    if nx > 2:
-        pl.semaphore_wait(ready.at[3], 2)
-    if len(steps_z) > 1:
-        reach_end(1)
-    if len(steps_z) > 2:
-        reach_start(2)
-
-    each(ny - 1, lambda i: y_copy(0, i + 1, st_send, st_buf.at[y_from(i + 1)]).wait_recv())
-    steps = st_buf[...].reshape(BLOCK, LANES)
+
+    y_copy(0, 1, some(sw_send, ny), some(sw_buf, ny)).wait_recv()
+    steps = sw_buf[:, :, 0:LANES].reshape(BLOCK, LANES)
+    wr = sw_buf[:, :, LANES:2 * LANES].reshape(BLOCK, LANES)
     pick = (lax.broadcasted_iota(jnp.int32, (LANES, HEADS_HERE * LANES), 0) == me * HEADS_HERE
             + lax.broadcasted_iota(jnp.int32, (LANES, HEADS_HERE * LANES), 1) // LANES)
     spread_steps = dot_nn(steps, jnp.where(pick, 1.0, 0.0).astype(BF16)).astype(BF16)
@@ -242,54 +234,44 @@
     for t in range(PAIRS):
         dec_send[t] = jnp.exp(pair_last(t)) * through
     dec_recv[zme] = dec_send[zme // blocks_of]
-
-    def send_decay(i):
-        k = z_offset(i)
+    reach_end(2)
+    for k in far_first(nz):
         z_copy(0, k, dec_send.at[lax.div(z_peer(k), blocks_of)], dec_recv.at[zme]).start()
 
-    if len(steps_z) > 2:
-        reach_end(2)
-    each(nz - 1, send_decay)
-
-    each(ny - 1, lambda i: y_copy(1, i + 1, wr_send.at[y_peer(i + 1)], wr_buf.at[y_from(i + 1)]).wait_recv())
-    wr = wr_buf[...].reshape(BLOCK, LANES)
+    for t in range(PAIRS):
+        cols = slice(t * LANES, (t + 1) * LANES)
+        fout_ref[:, cols] = factor_out(t)
+        fin_ref[:, cols] = factor_in(t)
     rw = pltpu.roll(wr.astype(F32), 64, 1)
     writers = wr[:, 0:64]
     readers = rw[:, 0:64].astype(BF16)
     read_low = jnp.where(low, rw, 0.0).astype(BF16)
     write_high = jnp.where(low, 0.0, rw).astype(BF16)
     score_ref[...] = dot_nt(readers, writers)
-
-    each(ny - 1, lambda i: y_copy(2, i + 1, x_in.at[:, wide(y_peer(i + 1))], v_buf.at[y_from(i + 1)]).wait_recv())
+    turned = jnp.transpose(wr.astype(F32)).astype(BF16)
+
+    y_copy(1, 1, some_wide(x_in), some(v_buf, ny)).wait_recv()
     for t in range(PAIRS):
         cols = slice(t * LANES, (t + 1) * LANES)
         values = v_buf[:, :, cols].reshape(BLOCK, LANES)
-        ev = (values.astype(F32) * factor_out(t)).astype(BF16)
+        ev = (values.astype(F32) * fout_ref[:, cols]).astype(BF16)
         ev_ref[:, cols] = ev
-        added = dot_tn(wr, ev)[0:STATE].astype(BF16)
+        added = dot_nn(turned[0:STATE], ev).astype(BF16)
         f_send[t * blocks_of:(t + 1) * blocks_of] = added.reshape(blocks_of, piece, LANES)
-
-    def send_f(i):
-        k = z_offset(i)
+    for k in far_first(nz):
         z_copy(1, k, f_send.at[z_peer(k)], f_recv.at[zme]).start()
-
-    each(nz - 1, send_f)
     f_recv[zme] = f_send[zme]
 
-    each(ny - 1, lambda i: y_copy(3, i + 1, g_in.at[:, wide(y_peer(i + 1))], g_buf.at[y_from(i + 1)]).wait_recv())
+    y_copy(2, 1, some_wide(g_in), some(g_buf, ny)).wait_recv()
     for t in range(PAIRS):
         cols = slice(t * LANES, (t + 1) * LANES)
         grads = g_buf[:, :, cols].reshape(BLOCK, LANES)
-        cg = (grads.astype(F32) * factor_in(t)).astype(BF16)
+        cg = (grads.astype(F32) * fin_ref[:, cols]).astype(BF16)
         cg_ref[:, cols] = cg
-        added = dot_tn(wr, cg)[STATE:2 * STATE].astype(BF16)
+        added = dot_nn(turned[STATE:2 * STATE], cg).astype(BF16)
         b_send[t * blocks_of:(t + 1) * blocks_of] = added.reshape(blocks_of, piece, LANES)
-
-    def send_b(i):
-        k = z_offset(i)
+    for k in far_first(nz):
         z_copy(2, k, b_send.at[z_peer(k)], b_recv.at[zme]).start()
-
-    each(nz - 1, send_b)
     b_recv[zme] = b_send[zme]
 
     low_one = jnp.where(low_row, 1.0, 0.0).astype(BF16)
@@ -317,8 +299,8 @@
 
     lax.fori_loop(0, 2, inside, 0)
 
-    each(nz - 1, lambda i: z_copy(0, i + 1, dec_send.at[0], dec_recv.at[z_from(i + 1)]).wait_recv())
-    each(nz - 1, lambda i: z_copy(1, i + 1, f_send.at[0], f_recv.at[z_from(i + 1)]).wait_recv())
+    z_copy(0, 1, some(dec_recv, nz), some(dec_recv, nz)).wait_recv()
+    z_copy(1, 1, some(f_send, nz), some(f_recv, nz)).wait_recv()
     total = jnp.zeros((piece, LANES), F32)
     product = jnp.ones((1, LANES), F32)
     for z in range(nz):
@@ -326,19 +308,21 @@
         product = dec_recv[z] * product
     xf_send[0:piece] = total
     xf_send[piece:piece + 8] = jnp.broadcast_to(product, (8, LANES))
-    each(nx - 1, lambda i: x_copy(0, i + 1, xf_send, xf_recv.at[xme]).start())
+    for k in far_first(nx):
+        x_copy(0, k, xf_send, xf_recv.at[xme]).start()
     xf_recv[xme] = xf_send[...]
-    each(nz - 1, lambda i: z_copy(2, i + 1, b_send.at[0], b_recv.at[z_from(i + 1)]).wait_recv())
+    z_copy(2, 1, some(b_send, nz), some(b_recv, nz)).wait_recv()
     total = jnp.zeros((piece, LANES), F32)
     for z in reversed(range(nz)):
         total = dec_recv[z] * total + b_recv[z].astype(F32)
     xb_send[...] = total
-    each(nx - 1, lambda i: x_copy(1, i + 1, xb_send, xb_recv.at[xme]).start())
+    for k in far_first(nx):
+        x_copy(1, k, xb_send, xb_recv.at[xme]).start()
     xb_recv[xme] = xb_send[...]
 
     lax.fori_loop(2, 3, inside, 0)
 
-    each(nx - 1, lambda i: x_copy(0, i + 1, xf_send, xf_recv.at[x_from(i + 1)]).wait_recv())
+    x_copy(0, 1, some(xf_recv, nx), some(xf_recv, nx)).wait_recv()
     state = jnp.zeros((piece, LANES), F32)
     for x in range(nx):
         longer = xf_recv[x, piece:piece + 1] * state + xf_recv[x, 0:piece]
@@ -346,15 +330,11 @@
     for z in range(nz):
         rf_send[z] = state.astype(BF16)
         state = dec_recv[z] * state + f_recv[z].astype(F32)
-
-    def return_f(i):
-        k = z_offset(i)
+    for k in far_first(nz):
         z_copy(3, k, rf_send.at[z_peer(k)], rf_recv.at[zme]).start()
-
-    each(nz - 1, return_f)
     rf_recv[zme] = rf_send[zme]
 
-    each(nx - 1, lambda i: x_copy(1, i + 1, xb_send, xb_recv.at[x_from(i + 1)]).wait_recv())
+    x_copy(1, 1, some(xb_recv, nx), some(xb_recv, nx)).wait_recv()
     state = jnp.zeros((piece, LANES), F32)
     for x in reversed(range(nx)):
         longer = xf_recv[x, piece:piece + 1] * state + xb_recv[x]
@@ -362,12 +342,8 @@
     for z in reversed(range(nz)):
         rb_send[z] = state.astype(BF16)
         state = dec_recv[z] * state + b_recv[z].astype(F32)
-
-    def return_b(i):
-        k = z_offset(i)
+    for k in far_first(nz):
         z_copy(4, k, rb_send.at[z_peer(k)], rb_recv.at[zme]).start()
-
-    each(nz - 1, return_b)
     rb_recv[zme] = rb_send[zme]
 
     lax.fori_loop(3, 4, inside, 0)
@@ -375,60 +351,51 @@
     gw = dot_nn(dscore, write_high) + dot_tn(dscore, read_low)
     nothing = jnp.zeros((STATE, LANES), BF16)
 
-    each(nz - 1, lambda i: z_copy(3, i + 1, rf_send.at[0], rf_recv.at[z_from(i + 1)]).wait_recv())
+    z_copy(3, 1, some(rf_send, nz), some(rf_recv, nz)).wait_recv()
     for t in range(PAIRS):
         cols = slice(t * LANES, (t + 1) * LANES)
         entering = rf_recv[t * blocks_of:(t + 1) * blocks_of].reshape(STATE, LANES)
-        result = loc_ref[:, cols] + factor_in(t) * dot_nn(readers, entering)
+        result = loc_ref[:, cols] + fin_ref[:, cols] * dot_nn(readers, entering)
         out_send[:, :, cols] = result.astype(BF16).reshape(ny, rows, LANES)
+    for k in far_first(ny):
+        y_copy(3, k, out_send.at[y_peer(k)], out_ref.at[:, wide(me)]).start()
+    out_ref[:, wide(me)] = out_send[me]
+    for t in range(PAIRS):
+        cols = slice(t * LANES, (t + 1) * LANES)
+        entering = rf_recv[t * blocks_of:(t + 1) * blocks_of].reshape(STATE, LANES)
         gw = gw + dot_nt(cg_ref[:, cols], jnp.concatenate([nothing, entering], axis=0))
-    each(ny - 1, lambda i: y_copy(4, i + 1, out_send.at[y_peer(i + 1)], out_ref.at[:, wide(me)]).start())
-    out_ref[:, wide(me)] = out_send[me]
-
-    each(nz - 1, lambda i: z_copy(4, i + 1, rb_send.at[0], rb_recv.at[z_from(i + 1)]).wait_recv())
+
+    z_copy(4, 1, some(rb_send, nz), some(rb_recv, nz)).wait_recv()
     for t in range(PAIRS):
         cols = slice(t * LANES, (t + 1) * LANES)
         leaving = rb_recv[t * blocks_of:(t + 1) * blocks_of].reshape(STATE, LANES)
-        result = dv_ref[:, cols] + factor_out(t) * dot_nn(writers, leaving)
+        result = dv_ref[:, cols] + fout_ref[:, cols] * dot_nn(writers, leaving)
         dx_send[:, :, cols] = result.astype(BF16).reshape(ny, rows, LANES)
+    for k in far_first(ny):
+        y_copy(4, k, dx_send.at[y_peer(k)], dx_ref.at[:, wide(me)]).start()
+    dx_ref[:, wide(me)] = dx_send[me]
+    for t in range(PAIRS):
+        cols = slice(t * LANES, (t + 1) * LANES)
+        leaving = rb_recv[t * blocks_of:(t + 1) * blocks_of].reshape(STATE, LANES)
         gw = gw + dot_nt(ev_ref[:, cols], jnp.concatenate([leaving, nothing], axis=0))
     gw_send[...] = gw.astype(BF16).reshape(ny, rows, LANES)
-    each(ny - 1, lambda i: y_copy(6, i + 1, gw_send.at[y_peer(i + 1)], gw_recv.at[me]).start())
-    each(ny - 1, lambda i: y_copy(5, i + 1, dx_send.at[y_peer(i + 1)], dx_ref.at[:, wide(me)]).start())
-    dx_ref[:, wide(me)] = dx_send[me]
+    for k in far_first(ny):
+        y_copy(5, k, gw_send.at[y_peer(k)], gw_recv.at[me]).start()
     gw_recv[me] = gw_send[me]
 
-    def drain_y(i):
-        k = i + 1
-        y_copy(0, k, st_send, st_buf.at[me]).wait_send()
-        y_copy(1, k, wr_send.at[y_peer(k)], wr_buf.at[me]).wait_send()
-        y_copy(2, k, x_in.at[:, wide(y_peer(k))], v_buf.at[me]).wait_send()
-        y_copy(3, k, g_in.at[:, wide(y_peer(k))], g_buf.at[me]).wait_send()
-
-    def drain_z(i):
-        k = i + 1
-        z_copy(0, k, dec_send.at[0], dec_recv.at[zme]).wait_send()
-        z_copy(1, k, f_send.at[z_peer(k)], f_recv.at[zme]).wait_send()
-        z_copy(2, k, b_send.at[z_peer(k)], b_recv.at[zme]).wait_send()
-        z_copy(3, k, rf_send.at[z_peer(k)], rf_recv.at[zme]).wait_send()
-        z_copy(4, k, rb_send.at[z_peer(k)], rb_recv.at[zme]).wait_send()
-
-    def drain_x(i):
-        k = i + 1
-        x_copy(0, k, xf_send, xf_recv.at[xme]).wait_send()
-        x_copy(1, k, xb_send, xb_recv.at[xme]).wait_send()
-
-    each(ny - 1, drain_y)
-    each(nz - 1, drain_z)
-    each(nx - 1, drain_x)
-
-    def finish(i):
-        k = i + 1
-        y_copy(4, k, out_send.at[y_peer(k)], out_ref.at[:, wide(y_from(k))]).wait()
-        y_copy(6, k, gw_send.at[y_peer(k)], gw_recv.at[y_from(k)]).wait()
-        y_copy(5, k, dx_send.at[y_peer(k)], dx_ref.at[:, wide(y_from(k))]).wait()
-
-    each(ny - 1, finish)
+    y_copy(0, 1, some(sw_send, ny), some(sw_buf, ny)).wait_send()
+    y_copy(1, 1, some_wide(x_in), some(v_buf, ny)).wait_send()
+    y_copy(2, 1, some_wide(g_in), some(g_buf, ny)).wait_send()
+    z_copy(0, 1, some(dec_recv, nz), some(dec_recv, nz)).wait_send()
+    z_copy(1, 1, some(f_send, nz), some(f_recv, nz)).wait_send()
+    z_copy(2, 1, some(b_send, nz), some(b_recv, nz)).wait_send()
+    z_copy(3, 1, some(rf_send, nz), some(rf_recv, nz)).wait_send()
+    z_copy(4, 1, some(rb_send, nz), some(rb_recv, nz)).wait_send()
+    x_copy(0, 1, some(xf_recv, nx), some(xf_recv, nx)).wait_send()
+    x_copy(1, 1, some(xb_recv, nx), some(xb_recv, nx)).wait_send()
+    y_copy(3, 1, some(out_send, ny), some_wide(out_ref)).wait()
+    y_copy(4, 1, some(dx_send, ny), some_wide(dx_ref)).wait()
+    y_copy(5, 1, some(gw_send, ny), some(gw_recv, ny)).wait()
 
 
 def last(ny, out_in, dx_in, gw_in, out_ref, dx_ref, dw_ref, dr_ref, dw_out, dr_out, sem):
@@ -471,7 +438,7 @@
         scratch_shapes=[
             bf(rows, ny * WIDE), bf(rows, ny * WIDE), bf(*step_sizes.shape), bf(*state_write.shape),
             bf(*state_read.shape), pltpu.SMEM(decay_rates.shape, F32), pltpu.SMEM((DOCS,), jnp.int32),
-            bf(rows, LANES), bf(ny, rows, LANES), bf(ny, rows, LANES), bf(ny, rows, LANES),
+            bf(ny, rows, 2 * LANES), bf(ny, rows, 2 * LANES),
             bf(ny, rows, WIDE), bf(ny, rows, WIDE),
             fl(PAIRS, 1, LANES), fl(nz, 1, LANES),
             bf(nz, piece, LANES), bf(nz, piece, LANES), bf(nz, piece, LANES), bf(nz, piece, LANES),
@@ -480,9 +447,10 @@
             bf(ny, rows, WIDE), bf(ny, rows, WIDE), bf(ny, rows, LANES),
             fl(BLOCK, HEADS_HERE * LANES), fl(HEADS_HERE, BLOCK), fl(BLOCK, BLOCK), fl(BLOCK, BLOCK),
             fl(BLOCK, BLOCK), bf(BLOCK, WIDE), bf(BLOCK, WIDE), fl(BLOCK, WIDE), fl(BLOCK, WIDE),
-            pltpu.SemaphoreType.DMA((7, ny)), pltpu.SemaphoreType.DMA((7, ny)),
-            pltpu.SemaphoreType.DMA((5, nz)), pltpu.SemaphoreType.DMA((5, nz)),
-            pltpu.SemaphoreType.DMA((2, nx)), pltpu.SemaphoreType.DMA((2, nx)),
+            fl(BLOCK, WIDE), fl(BLOCK, WIDE),
+            pltpu.SemaphoreType.DMA((6,)), pltpu.SemaphoreType.DMA((6,)),
+            pltpu.SemaphoreType.DMA((5,)), pltpu.SemaphoreType.DMA((5,)),
+            pltpu.SemaphoreType.DMA((2,)), pltpu.SemaphoreType.DMA((2,)),
             pltpu.SemaphoreType.DMA((7,)), pltpu.SemaphoreType.REGULAR((4,)),
         ],
         compiler_params=pltpu.CompilerParams(collective_id=0, has_side_effects=True),

time: 52.1 us -> 49.8 us (0.956)
  Pallas kernels: 51.4 us -> 49 us
    pallas_call x1, Pallas kernels: 50.5 us -> 48.2 us  [on_device(): pl.pallas_call(functools.partial(kernel, nx, nz, ny), out_shape=(bf(*inpu...]
where the time goes in v3:
time: 49.8 us; the launch traced here: 49.6 us
  Pallas kernels  49 us (98%)
  between operations  0.64 us (1%)
    pallas_call x1, Pallas kernels, on_device(): pl.pallas_call(functools.partial(kernel, nx, nz, ny), out_shape=(bf(*inpu...  48.2 us

profile of v3, /device:TPU:1, one launch (start us, length us, event | category | flops | bytes accessed | tf_op | source)
XLA Modules:
  0.0 49.6 jit_solution(11965077449029638078)
XLA Ops:
  0.6 48.2 %shard_map.102 = (bf16[32,4096]{1,0:T(8,128)(2,1)S(1)}, bf16[32,4096]{1,0:T(8,128)(2,1)S(1)}, bf16[8,32,128]{2,1,0:T(8,128)(2,1)S(1)}) custom-call(bf16[32,4096]{1,0:T(8,128)(2,1)} %x_ref.1, bf16[32,64]{1,0:T(8,128)(2,1)} %step_ref.1, f32[8]{0:T(128)} %rate_ref.1, bf16[32,512]{1,0:T(8,128)(2,1)} %w_ref.1, bf16[32,512]{1,0:T(8,128)(2,1)} %r_ref.1, ...), custom_call_target="tpu_custom_call" | custom-call | tf_op jit(solution)/shard_map/pallas_call | solution.py:433
  48.8 0.8 %shard_map.103 = (bf16[32,4096]{1,0:T(8,128)(2,1)}, bf16[32,4096]{1,0:T(8,128)(2,1)}, bf16[32,512]{1,0:T(8,128)(2,1)}, bf16[32,512]{1,0:T(8,128)(2,1)}) custom-call(bf16[32,4096]{1,0:T(8,128)(2,1)S(1)} %get-tuple-element.7.out_in, bf16[32,4096]{1,0:T(8,128)(2,1)S(1)} %get-tuple-element.8.dx_in, bf16[8,32,128]{2,1,0:T(8,128)(2,1)S(1)} %get-tuple-element.9.gw_in), custom_call_target="tpu_custom_call" | custom-call | tf_op jit(solution)/shard_map/pallas_call | solution.py:458

commit v4 on v3

--- a/solution.py
+++ b/solution.py
@@ -36,7 +36,7 @@
     nx, nz, ny,
     x_ref, step_ref, rate_ref, w_ref, r_ref, doc_ref, g_ref,
     out_ref, dx_ref, gw_recv,
-    x_in, g_in, step_in, w_in, r_in, rate_in, doc_in,
+    step_in, w_in, r_in, rate_in, doc_in,
     sw_send, sw_buf, v_buf, g_buf,
     dec_send, dec_recv, f_send, f_recv, b_send, b_recv,
     xf_send, xf_recv, xb_send, xb_recv,
@@ -96,6 +96,9 @@
     def far_first(n):
         return sorted(range(1, n), key=lambda k: (-min(k, n - k), k))
 
+    def near_first(n):
+        return far_first(n)[::-1]
+
     def some(ref, n):
         return ref.at[pl.ds(0, n - 1)]
 
@@ -114,7 +117,8 @@
     fetch = [
         pltpu.make_async_copy(src, dst, own_sem.at[i])
         for i, (src, dst) in enumerate((
-            (step_ref, step_in), (w_ref, w_in), (r_ref, r_in), (x_ref, x_in), (g_ref, g_in),
+            (step_ref, step_in), (w_ref, w_in), (r_ref, r_in), (x_ref.at[:, wide(me)], v_buf.at[me]),
+            (g_ref.at[:, wide(me)], g_buf.at[me]),
             (doc_ref, doc_in), (rate_ref, rate_in)))
     ]
     for copy in fetch:
@@ -134,7 +138,6 @@
         sw_send[2 * pair + 1, :, 0:LANES] = steps_here
         sw_send[2 * pair, :, LANES:2 * LANES] = jnp.where(low, w2, pltpu.roll(r2, 64, 1)).astype(BF16)
         sw_send[2 * pair + 1, :, LANES:2 * LANES] = jnp.where(low, pltpu.roll(w2, 64, 1), r2).astype(BF16)
-    fetch[3].wait()
     pl.semaphore_wait(barrier, ny - 1 + len(x_near) + 2)
 
     steps_z = []
@@ -157,15 +160,14 @@
         signal_x(ready.at[3], 1)
         signal_x(ready.at[3], nx - 1)
 
-    for k in far_first(ny):
+    for k in near_first(ny):
         y_copy(0, k, sw_send.at[y_peer(k)], sw_buf.at[me]).start()
-    for k in far_first(ny):
-        y_copy(1, k, x_in.at[:, wide(y_peer(k))], v_buf.at[me]).start()
+    for k in near_first(ny):
+        y_copy(1, k, x_ref.at[:, wide(y_peer(k))], v_buf.at[me]).start()
     reach_end(0)
     reach_start(1)
-    fetch[4].wait()
-    for k in far_first(ny):
-        y_copy(2, k, g_in.at[:, wide(y_peer(k))], g_buf.at[me]).start()
+    for k in near_first(ny):
+        y_copy(2, k, g_ref.at[:, wide(y_peer(k))], g_buf.at[me]).start()
 
     fetch[5].wait()
     fetch[6].wait()
@@ -189,8 +191,8 @@
         pl.semaphore_wait(ready.at[3], 2)
     reach_end(1)
     reach_start(2)
-    v_buf[me] = x_in[:, wide(me)]
-    g_buf[me] = g_in[:, wide(me)]
+    fetch[3].wait()
+    fetch[4].wait()
     sw_buf[me] = sw_send[me]
     row_i = lax.broadcasted_iota(jnp.int32, (BLOCK, BLOCK), 0)
     col_i = lax.broadcasted_iota(jnp.int32, (BLOCK, BLOCK), 1)
@@ -250,7 +252,7 @@
     score_ref[...] = dot_nt(readers, writers)
     turned = jnp.transpose(wr.astype(F32)).astype(BF16)
 
-    y_copy(1, 1, some_wide(x_in), some(v_buf, ny)).wait_recv()
+    y_copy(1, 1, some_wide(x_ref), some(v_buf, ny)).wait_recv()
     for t in range(PAIRS):
         cols = slice(t * LANES, (t + 1) * LANES)
         values = v_buf[:, :, cols].reshape(BLOCK, LANES)
@@ -262,7 +264,7 @@
         z_copy(1, k, f_send.at[z_peer(k)], f_recv.at[zme]).start()
     f_recv[zme] = f_send[zme]
 
-    y_copy(2, 1, some_wide(g_in), some(g_buf, ny)).wait_recv()
+    y_copy(2, 1, some_wide(g_ref), some(g_buf, ny)).wait_recv()
     for t in range(PAIRS):
         cols = slice(t * LANES, (t + 1) * LANES)
         grads = g_buf[:, :, cols].reshape(BLOCK, LANES)
@@ -297,7 +299,7 @@
         dv_ref[:, cols] = dvalue
         return carry
 
-    lax.fori_loop(0, 2, inside, 0)
+    lax.fori_loop(0, 4, inside, 0)
 
     z_copy(0, 1, some(dec_recv, nz), some(dec_recv, nz)).wait_recv()
     z_copy(1, 1, some(f_send, nz), some(f_recv, nz)).wait_recv()
@@ -320,7 +322,6 @@
         x_copy(1, k, xb_send, xb_recv.at[xme]).start()
     xb_recv[xme] = xb_send[...]
 
-    lax.fori_loop(2, 3, inside, 0)
 
     x_copy(0, 1, some(xf_recv, nx), some(xf_recv, nx)).wait_recv()
     state = jnp.zeros((piece, LANES), F32)
@@ -346,7 +347,6 @@
         z_copy(4, k, rb_send.at[z_peer(k)], rb_recv.at[zme]).start()
     rb_recv[zme] = rb_send[zme]
 
-    lax.fori_loop(3, 4, inside, 0)
     dscore = dscore_ref[...].astype(BF16)
     gw = dot_nn(dscore, write_high) + dot_tn(dscore, read_low)
     nothing = jnp.zeros((STATE, LANES), BF16)
@@ -384,8 +384,8 @@
     gw_recv[me] = gw_send[me]
 
     y_copy(0, 1, some(sw_send, ny), some(sw_buf, ny)).wait_send()
-    y_copy(1, 1, some_wide(x_in), some(v_buf, ny)).wait_send()
-    y_copy(2, 1, some_wide(g_in), some(g_buf, ny)).wait_send()
+    y_copy(1, 1, some_wide(x_ref), some(v_buf, ny)).wait_send()
+    y_copy(2, 1, some_wide(g_ref), some(g_buf, ny)).wait_send()
     z_copy(0, 1, some(dec_recv, nz), some(dec_recv, nz)).wait_send()
     z_copy(1, 1, some(f_send, nz), some(f_recv, nz)).wait_send()
     z_copy(2, 1, some(b_send, nz), some(b_recv, nz)).wait_send()
@@ -436,7 +436,7 @@
         in_specs=[anywhere] * 7,
         out_specs=(vmem, vmem, vmem),
         scratch_shapes=[
-            bf(rows, ny * WIDE), bf(rows, ny * WIDE), bf(*step_sizes.shape), bf(*state_write.shape),
+            bf(*step_sizes.shape), bf(*state_write.shape),
             bf(*state_read.shape), pltpu.SMEM(decay_rates.shape, F32), pltpu.SMEM((DOCS,), jnp.int32),
             bf(ny, rows, 2 * LANES), bf(ny, rows, 2 * LANES),
             bf(ny, rows, WIDE), bf(ny, rows, WIDE),

time: 49.8 us -> 48.7 us (0.978)
  Pallas kernels: 49 us -> 47.8 us
    pallas_call x1, Pallas kernels: 48.2 us -> 47 us  [on_device(): pl.pallas_call(functools.partial(kernel, nx, nz, ny), out_shape=(bf(*inpu...]
where the time goes in v4:
time: 48.7 us; the launch traced here: 48.5 us
  Pallas kernels  47.8 us (98%)
  between operations  0.64 us (1%)
    pallas_call x1, Pallas kernels, on_device(): pl.pallas_call(functools.partial(kernel, nx, nz, ny), out_shape=(bf(*inpu...  47 us

profile of v4, /device:TPU:1, one launch (start us, length us, event | category | flops | bytes accessed | tf_op | source)
XLA Modules:
  0.0 48.5 jit_solution(2660468069952264950)
XLA Ops:
  0.6 47.0 %shard_map.102 = (bf16[32,4096]{1,0:T(8,128)(2,1)S(1)}, bf16[32,4096]{1,0:T(8,128)(2,1)S(1)}, bf16[8,32,128]{2,1,0:T(8,128)(2,1)S(1)}) custom-call(bf16[32,4096]{1,0:T(8,128)(2,1)} %x_ref.1, bf16[32,64]{1,0:T(8,128)(2,1)} %step_ref.1, f32[8]{0:T(128)} %rate_ref.1, bf16[32,512]{1,0:T(8,128)(2,1)} %w_ref.1, bf16[32,512]{1,0:T(8,128)(2,1)} %r_ref.1, ...), custom_call_target="tpu_custom_call" | custom-call | tf_op jit(solution)/shard_map/pallas_call | solution.py:433
  47.7 0.8 %shard_map.103 = (bf16[32,4096]{1,0:T(8,128)(2,1)}, bf16[32,4096]{1,0:T(8,128)(2,1)}, bf16[32,512]{1,0:T(8,128)(2,1)}, bf16[32,512]{1,0:T(8,128)(2,1)}) custom-call(bf16[32,4096]{1,0:T(8,128)(2,1)S(1)} %get-tuple-element.7.out_in, bf16[32,4096]{1,0:T(8,128)(2,1)S(1)} %get-tuple-element.8.dx_in, bf16[8,32,128]{2,1,0:T(8,128)(2,1)S(1)} %get-tuple-element.9.gw_in), custom_call_target="tpu_custom_call" | custom-call | tf_op jit(solution)/shard_map/pallas_call | solution.py:458

commit v5 on v4

--- a/solution.py
+++ b/solution.py
@@ -236,9 +236,6 @@
     for t in range(PAIRS):
         dec_send[t] = jnp.exp(pair_last(t)) * through
     dec_recv[zme] = dec_send[zme // blocks_of]
-    reach_end(2)
-    for k in far_first(nz):
-        z_copy(0, k, dec_send.at[lax.div(z_peer(k), blocks_of)], dec_recv.at[zme]).start()
 
     for t in range(PAIRS):
         cols = slice(t * LANES, (t + 1) * LANES)
@@ -251,6 +248,10 @@
     write_high = jnp.where(low, 0.0, rw).astype(BF16)
     score_ref[...] = dot_nt(readers, writers)
     turned = jnp.transpose(wr.astype(F32)).astype(BF16)
+
+    reach_end(2)
+    for k in far_first(nz):
+        z_copy(0, k, dec_send.at[lax.div(z_peer(k), blocks_of)], dec_recv.at[zme]).start()
 
     y_copy(1, 1, some_wide(x_ref), some(v_buf, ny)).wait_recv()
     for t in range(PAIRS):

time: 48.7 us -> 48.5 us (level)
  no operation moved by 1% of the time
where the time goes in v5:
time: 48.5 us; the launch traced here: 48.3 us
  Pallas kernels  47.7 us (98%)
  between operations  0.64 us (1%)
    pallas_call x1, Pallas kernels, on_device(): pl.pallas_call(functools.partial(kernel, nx, nz, ny), out_shape=(bf(*inpu...  46.9 us

profile of v5, /device:TPU:1, one launch (start us, length us, event | category | flops | bytes accessed | tf_op | source)
XLA Modules:
  0.0 48.3 jit_solution(5404649571755142478)
XLA Ops:
  0.6 46.9 %shard_map.102 = (bf16[32,4096]{1,0:T(8,128)(2,1)S(1)}, bf16[32,4096]{1,0:T(8,128)(2,1)S(1)}, bf16[8,32,128]{2,1,0:T(8,128)(2,1)S(1)}) custom-call(bf16[32,4096]{1,0:T(8,128)(2,1)} %x_ref.1, bf16[32,64]{1,0:T(8,128)(2,1)} %step_ref.1, f32[8]{0:T(128)} %rate_ref.1, bf16[32,512]{1,0:T(8,128)(2,1)} %w_ref.1, bf16[32,512]{1,0:T(8,128)(2,1)} %r_ref.1, ...), custom_call_target="tpu_custom_call" | custom-call | tf_op jit(solution)/shard_map/pallas_call | solution.py:434
  47.5 0.8 %shard_map.103 = (bf16[32,4096]{1,0:T(8,128)(2,1)}, bf16[32,4096]{1,0:T(8,128)(2,1)}, bf16[32,512]{1,0:T(8,128)(2,1)}, bf16[32,512]{1,0:T(8,128)(2,1)}) custom-call(bf16[32,4096]{1,0:T(8,128)(2,1)S(1)} %get-tuple-element.7.out_in, bf16[32,4096]{1,0:T(8,128)(2,1)S(1)} %get-tuple-element.8.dx_in, bf16[8,32,128]{2,1,0:T(8,128)(2,1)S(1)} %get-tuple-element.9.gw_in), custom_call_target="tpu_custom_call" | custom-call | tf_op jit(solution)/shard_map/pallas_call | solution.py:459
